TPU v7x, 32 devices: a whole 2x2x4 slice. The times are simulated.
32 devices in a mesh: query: 8 (over z, y), item: 4 (over x, core).
Axes of the slice: x: 2, y: 2, z: 4, core: 2. Of those that a mesh axis runs over, the one named last changes fastest.
Arguments:
- query_emb: bfloat16 [2048, 256], P(('query', 'item')), may hold values from -400 to 400
- targets: int32 [2048], P('query'), may hold values from 0 to 8191, as said below
- eligible_tiles: int32 [32, 32], P('query', 'item'), may hold values from 0 to 1, as said below
- item_feats: bfloat16 [4, 2048, 512], P('item', 'query'), may hold values from -6 to 6
- w_first: bfloat16 [512, 1024], replicated, may hold values from -0.25 to 0.25
- w_second: bfloat16 [1024, 256], replicated, may hold values from -0.1875 to 0.1875
Outputs:
- loss: float32 [2048], P(('query', 'item'))
- query_grad: float32 [2048, 256], P(('query', 'item'))
- w_first_grad: float32 [512, 1024], replicated
- w_second_grad: float32 [1024, 256], replicated
Inputs may be any that keep to these rules, and one draw needn't show every extreme that they name: `eligible_tiles`: every row has at least one 1. The block targets[q] // 256 is marked 1 in row q // 64 of eligible_tiles.
All inputs are finite; a program needn't handle non-finite values.
Results may differ from a plain program's by a relative error of at most 0.007.
Values may be sent and summed in bfloat16 or wider, within the bound.
A program may use at most 64 MiB of HBM per device.

v0:
```python
import math

import jax
import jax.numpy as jnp
from jax import lax
from jax.sharding import PartitionSpec as P


def passed_along(x, axis, by):
    count = lax.axis_size(axis)
    return lax.ppermute(x, axis, [(i, (i + by) % count) for i in range(count)])


def expand_blocks(block_flags, per_block):
    widened = jnp.broadcast_to((block_flags > 0)[..., None], block_flags.shape + (per_block,))
    return widened.reshape(block_flags.shape[:-1] + (block_flags.shape[-1] * per_block,))


def tile_scores(queries, item_tile):
    return 0.25 * jnp.einsum("qe,ie->qi", queries, item_tile, preferred_element_type=jnp.float32)


def on_device(query_emb, targets, eligible_tiles, item_feats, w_first, w_second):
    q_rows = query_emb.shape[0]
    item_count = lax.axis_size("item")
    query_count = lax.axis_size("query")
    item_pos = lax.axis_index("item")
    tokens = item_feats.reshape(item_feats.shape[1], item_feats.shape[2])
    block_rows = tokens.shape[0]
    pre_act = jnp.dot(tokens, w_first, preferred_element_type=jnp.float32)
    hidden = jax.nn.silu(pre_act).astype(jnp.bfloat16)
    own_emb = jnp.dot(hidden, w_second, preferred_element_type=jnp.float32).astype(jnp.bfloat16)
    item_tile = lax.all_gather(own_emb, "query", axis=0, tiled=True)
    tile_rows = item_tile.shape[0]
    emb_width = item_tile.shape[1]
    columns = jnp.arange(tile_rows, dtype=jnp.int32)
    first_item = item_pos * tile_rows
    start_cache = jnp.zeros((1, 1, 1), jnp.bfloat16)

    def forward_step(step_idx, carried):
        visitor, run_max, run_sum, positive, seen = carried
        anchor = (item_pos - step_idx) % item_count
        live_cols = expand_blocks(
            lax.dynamic_index_in_dim(eligible_tiles, anchor, 0, keepdims=False), block_rows
        )[None, :]
        wanted = lax.dynamic_slice_in_dim(targets, anchor * q_rows, q_rows, 0) - first_item
        queries = visitor.astype(jnp.bfloat16)
        scores = tile_scores(queries, item_tile)
        masked = jnp.where(live_cols, scores, -1e30)
        new_max = jnp.maximum(run_max, jnp.max(masked, axis=1))
        added = jnp.sum(jnp.where(live_cols, jnp.exp(masked - new_max[:, None]), 0.0), axis=1)
        run_sum = run_sum * jnp.exp(run_max - new_max) + added
        positive = positive + jnp.sum(
            jnp.where(columns[None, :] == wanted[:, None], scores, 0.0), axis=1
        )
        moved = passed_along((visitor, new_max, run_sum, positive), "item", 1)
        return (moved[0], moved[1], moved[2], moved[3], seen)

    start_state = (
        query_emb.astype(jnp.float32),
        jnp.full((q_rows,), -1e30, jnp.float32),
        jnp.zeros((q_rows,), jnp.float32),
        jnp.zeros((q_rows,), jnp.float32),
        start_cache,
    )
    visitor, run_max, run_sum, positive, seen = lax.fori_loop(
        0, item_count, forward_step, start_state
    )
    log_norm = run_max + jnp.log(run_sum)
    loss = log_norm - positive

    def tile_grads(queries, norm_here, step_idx):
        anchor = (item_pos - step_idx) % item_count
        live_cols = expand_blocks(
            lax.dynamic_index_in_dim(eligible_tiles, anchor, 0, keepdims=False), block_rows
        )[None, :]
        wanted = lax.dynamic_slice_in_dim(targets, anchor * q_rows, q_rows, 0) - first_item
        masked = jnp.where(live_cols, tile_scores(queries, item_tile), -1e30)
        softmax_w = jnp.where(live_cols, jnp.exp(masked - norm_here[:, None]), 0.0)
        coeffs = (softmax_w - (columns[None, :] == wanted[:, None]).astype(jnp.float32)).astype(
            jnp.bfloat16
        )
        q_part = 0.25 * jnp.dot(coeffs, item_tile, preferred_element_type=jnp.float32)
        e_part = 0.25 * jnp.einsum("qi,qe->ie", coeffs, queries, preferred_element_type=jnp.float32)
        return (q_part, e_part)

    zero_q = jnp.zeros((q_rows, emb_width), jnp.float32)
    zero_e = jnp.zeros(item_tile.shape, jnp.float32)

    def backward_step(step_idx, carried):
        travel, emb_grad = carried
        visitor, norm_here, q_grads = travel
        q_part, e_part = tile_grads(visitor.astype(jnp.bfloat16), norm_here, step_idx)
        travel = passed_along((visitor, norm_here, q_grads + q_part), "item", 1)
        return (travel, emb_grad + e_part)

    start_back = ((query_emb.astype(jnp.float32), log_norm, zero_q), zero_e)
    travel, emb_grad = lax.fori_loop(0, item_count, backward_step, start_back)
    query_grad = travel[2]
    own_grad = lax.psum_scatter(emb_grad, "query", scatter_dimension=0, tiled=True).astype(
        jnp.bfloat16
    )
    second_term = jnp.einsum("ih,ie->he", hidden, own_grad, preferred_element_type=jnp.float32)
    hid_grad = jnp.einsum("ie,he->ih", own_grad, w_second, preferred_element_type=jnp.float32)
    gate_sig = jax.nn.sigmoid(pre_act)
    pre_grad = (hid_grad * gate_sig * (1.0 + pre_act * (1.0 - gate_sig))).astype(jnp.bfloat16)
    first_term = jnp.einsum("id,ih->dh", tokens, pre_grad, preferred_element_type=jnp.float32)
    tower_sums = lax.psum((first_term, second_term), ("query", "item"))
    grad_scale = 1.0 / math.sqrt(block_rows * query_count * item_count)
    return (loss, query_grad, tower_sums[0] * grad_scale, tower_sums[1] * grad_scale)


def solution(mesh):
    return jax.shard_map(
        on_device,
        mesh=mesh,
        in_specs=(
            P(("query", "item"), None),
            P("query"),
            P("query", "item"),
            P("item", "query", None),
            P(),
            P(),
        ),
        out_specs=(P(("query", "item")), P(("query", "item"), None), P(), P()),
        check_vma=False,
    )
```

profile of v0, /device:TPU:0, one launch (start us, length us, event | category | flops | bytes accessed | tf_op | source)
XLA Modules:
  0.0 334.7 jit_solution(5722697712973858926)
XLA Ops:
  7.2 0.9 copy.45
  8.4 1.4 fusion.22
  9.8 1.0 copy-done.2
  10.8 1.1 convolution_convert_fusion
  12.0 42.9 %all-gather.2.cloned.1.call-done = bf16[2048,256]{1,0:T(8,128)(2,1)} async-done(((bf16[256,256]{1,0:T(8,128)(2,1)}), bf16[2048,256]{1,0:T(8,128)(2,1)}) %all-gather.2.cloned.1.call-update) | async-done | bytes 1048592 | tf_op jit(solution)/shard_map/all_gather | solution.py:33
  54.9 26.8 %while.44 = (s32[]{:T(128)}, bf16[64,256]{1,0:T(8,128)(2,1)S(1)}, f32[64]{0:T(128)S(1)}, f32[64]{0:T(128)S(1)}, f32[64]{0:T(128)S(1)}, /*index=5*/s32[]{:T(128)}...) while((s32[]{:T(128)}, bf16[64,256]{1,0:T(8,128)(2,1)S(1)}, ...), condition=%wide.region_4.5_spmd.clone, body=%wide.region_0.4_spmd.clone.sunk | while | flops 68419800 | bytes 2345530 | solution.py:66
  55.1 1.8 select_reduce_fusion.5
  56.9 1.6 collective-permute-start.1
  59.0 0.6 collective-permute-start.3
  59.9 2.0 collective-permute-done.2
  62.3 1.8 select_reduce_fusion.5
  64.1 0.7 collective-permute-start.1
  65.3 1.5 collective-permute-start.3
  67.1 1.1 collective-permute-done.2
  68.5 1.8 select_reduce_fusion.5
  70.3 1.6 collective-permute-start.1
  72.0 0.3 select_reduce_fusion.6
  72.4 0.6 collective-permute-start.3
  73.3 2.0 collective-permute-done.2
  75.7 1.8 select_reduce_fusion.5
  77.4 0.7 collective-permute-start.1
  78.2 0.3 select_reduce_fusion.6
  78.6 1.5 collective-permute-start.3
  80.5 1.1 collective-permute-done.2
  81.7 0.5 fusion.29
  82.3 29.5 %while.45 = (s32[]{:T(128)}, bf16[64,256]{1,0:T(8,128)(2,1)S(1)}, f32[64]{0:T(128)S(1)}, f32[64,256]{1,0:T(8,128)S(1)}, f32[2048,256]{1,0:T(8,128)}, /*index=5*/...) while((s32[]{:T(128)}, bf16[64,256]{1,0:T(8,128)(2,1)S(1)}, ...), condition=%wide.region_6.7_spmd.clone, body=%wide.region_5.6_spmd.clone.sunk | while | flops 203980896 | bytes 11938872 | solution.py:98
  82.4 1.6 collective-permute-start.5
  84.1 1.7 fusion.60
  86.2 1.8 fusion.62
  88.0 1.8 collective-permute-done.6
  89.9 0.7 collective-permute-start.5
  90.7 1.7 fusion.60
  92.9 3.4 %fusion.62 = f32[2048,256]{1,0:T(8,128)} fusion(bf16[64,2048]{1,0:T(8,128)(2,1)S(1)} %fusion.60, f32[2048,256]{1,0:T(8,128)} %get-tuple-element.849, pred[]{:T(512)S(6)} %compare.5, bf16[64,256]{1,0:T(8,128)(2,1)S(1)} %copy.32), kind=kOutput, calls=%fused_computation.12.clone.1 | convolution fusion | flops 68681728 | bytes 4489217 | tf_op jit(solution)/shard_map/while/body/eval_jaxpr/qi,qe->ie/dot_general | solution.py:84
  96.5 1.4 collective-permute-start.4
  98.3 1.7 fusion.60
  100.3 0.5 collective-permute-start.6
  100.8 3.4 %fusion.62 = f32[2048,256]{1,0:T(8,128)} fusion(bf16[64,2048]{1,0:T(8,128)(2,1)S(1)} %fusion.60, f32[2048,256]{1,0:T(8,128)} %get-tuple-element.849, pred[]{:T(512)S(6)} %compare.5, bf16[64,256]{1,0:T(8,128)(2,1)S(1)} %copy.32), kind=kOutput, calls=%fused_computation.12.clone.1 | convolution fusion | flops 68681728 | bytes 4489217 | tf_op jit(solution)/shard_map/while/body/eval_jaxpr/qi,qe->ie/dot_general | solution.py:84
  104.5 1.4 collective-permute-start.5
  106.0 1.7 fusion.60
  108.3 3.4 %fusion.62 = f32[2048,256]{1,0:T(8,128)} fusion(bf16[64,2048]{1,0:T(8,128)(2,1)S(1)} %fusion.60, f32[2048,256]{1,0:T(8,128)} %get-tuple-element.849, pred[]{:T(512)S(6)} %compare.5, bf16[64,256]{1,0:T(8,128)(2,1)S(1)} %copy.32), kind=kOutput, calls=%fused_computation.12.clone.1 | convolution fusion | flops 68681728 | bytes 4489217 | tf_op jit(solution)/shard_map/while/body/eval_jaxpr/qi,qe->ie/dot_general | solution.py:84
  111.8 66.9 %reduce-scatter.2.cloned.1.call-done = f32[256,256]{1,0:T(8,128)} async-done(((f32[2048,256]{1,0:T(8,128)}), f32[256,256]{1,0:T(8,128)}) %reduce-scatter.2.cloned.1.call-update) | async-done | bytes 262160 | tf_op jit(solution)/shard_map/reduce_scatter | solution.py:100
  178.7 3.2 convolution_bitcast_fusion
  181.9 1.5 fusion.24
  183.4 138.1 %all-reduce.3.cloned.1.call-done = (f32[512,1024]{0,1:T(8,128)}, f32[1024,256]{1,0:T(8,128)}) async-done(((f32[512,1024]{0,1:T(8,128)}, f32[1024,256]{1,0:T(8,128)}), (f32[512,1024]{0,1:T(8,128)}, f32[1024,256]{1,0:T(8,128)})) %all-reduce.3.cloned.1.call-update) | async-done | bytes 3145744 | tf_op jit(solution)/shard_map/psum | solution.py:108
  321.6 1.8 broadcast_multiply_fusion
  323.4 1.8 copy.10
  325.2 2.3 broadcast_multiply_fusion.1
  327.5 0.6 copy.46
  (139 shorter events, 7.5 us)
Async XLA Ops:
  7.2 1.2 copy-start
  7.2 3.6 %copy-start.6 = (bf16[1024,256]{1,0:T(8,128)(2,1)S(1)}, bf16[1024,256]{1,0:T(8,128)(2,1)}, u32[]{:S(2)}) copy-start(bf16[1024,256]{1,0:T(8,128)(2,1)} %param.15) | copy-start | bytes 1572868
  7.2 47.7 %all-gather.2.cloned.1.call-start = ((), (), s32[]{:S(2)}) async-start(), calls=%async_computation.1 | async-start | bytes 1179648 | tf_op jit(solution)/shard_map/all_gather | solution.py:33
  9.8 1.0 copy-start.2
  10.8 44.1 %copy-start.5 = (s32[256]{0:T(256)S(1)}, s32[256]{0:T(256)}, u32[]{:S(2)}) copy-start(s32[256]{0:T(256)} %param.11) | copy-start | bytes 3076
  10.8 44.1 %copy-start.8 = (s32[4,8]{1,0:T(4,128)S(1)}, s32[4,8]{1,0:T(4,128)}, u32[]{:S(2)}) copy-start(s32[4,8]{1,0:T(4,128)} %param.12) | copy-start | bytes 388
  11.9 166.8 %reduce-scatter.2.cloned.1.call-start = ((), (), s32[]{:S(2)}) async-start(), calls=%async_computation.2 | async-start | bytes 2359296 | tf_op jit(solution)/shard_map/reduce_scatter | solution.py:100
  54.9 7.2 %collective-permute-start = (bf16[64,256]{1,0:T(8,128)(2,1)S(1)}, bf16[64,256]{1,0:T(8,128)(2,1)S(1)}, u32[]{:S(2)}, u32[]{:S(2)}) collective-permute-start(bf16[64,256]{1,0:T(8,128)(2,1)S(1)} %copy.17), channel_id=1, source_target_pairs={{0,1},{1,2},{2,3},{3,0},{4,5},{5,6},{6,7},{7,4},{8,9},{9,10},{10,1... | collective-permute-start | bytes 98312 | tf_op jit(solution)/shard_map/while/body/eval_jaxpr/ppermute | solution.py:11
  56.9 3.0 collective-permute-start.1
  58.9 3.0 collective-permute-start.2
  59.0 3.1 collective-permute-start.3
  62.1 6.2 %collective-permute-start = (bf16[64,256]{1,0:T(8,128)(2,1)S(1)}, bf16[64,256]{1,0:T(8,128)(2,1)S(1)}, u32[]{:S(2)}, u32[]{:S(2)}) collective-permute-start(bf16[64,256]{1,0:T(8,128)(2,1)S(1)} %copy.17), channel_id=1, source_target_pairs={{0,1},{1,2},{2,3},{3,0},{4,5},{5,6},{6,7},{7,4},{8,9},{9,10},{10,1... | collective-permute-start | bytes 98312 | tf_op jit(solution)/shard_map/while/body/eval_jaxpr/ppermute | solution.py:11
  64.1 3.0 collective-permute-start.1
  65.2 3.0 collective-permute-start.2
  65.3 3.1 collective-permute-start.3
  68.4 7.1 %collective-permute-start = (bf16[64,256]{1,0:T(8,128)(2,1)S(1)}, bf16[64,256]{1,0:T(8,128)(2,1)S(1)}, u32[]{:S(2)}, u32[]{:S(2)}) collective-permute-start(bf16[64,256]{1,0:T(8,128)(2,1)S(1)} %copy.17), channel_id=1, source_target_pairs={{0,1},{1,2},{2,3},{3,0},{4,5},{5,6},{6,7},{7,4},{8,9},{9,10},{10,1... | collective-permute-start | bytes 98312 | tf_op jit(solution)/shard_map/while/body/eval_jaxpr/ppermute | solution.py:11
  70.3 3.0 collective-permute-start.1
  72.3 3.0 collective-permute-start.2
  72.4 3.1 collective-permute-start.3
  75.5 6.2 %collective-permute-start = (bf16[64,256]{1,0:T(8,128)(2,1)S(1)}, bf16[64,256]{1,0:T(8,128)(2,1)S(1)}, u32[]{:S(2)}, u32[]{:S(2)}) collective-permute-start(bf16[64,256]{1,0:T(8,128)(2,1)S(1)} %copy.17), channel_id=1, source_target_pairs={{0,1},{1,2},{2,3},{3,0},{4,5},{5,6},{6,7},{7,4},{8,9},{9,10},{10,1... | collective-permute-start | bytes 98312 | tf_op jit(solution)/shard_map/while/body/eval_jaxpr/ppermute | solution.py:11
  77.4 3.0 collective-permute-start.1
  78.6 3.0 collective-permute-start.2
  78.6 3.1 collective-permute-start.3
  82.3 3.5 %copy-start.1 = (bf16[2048,256]{1,0:T(8,128)(2,1)S(1)}, bf16[2048,256]{1,0:T(8,128)(2,1)}, u32[]{:S(2)}) copy-start(bf16[2048,256]{1,0:T(8,128)(2,1)} %get-tuple-element.868) | copy-start | bytes 3145732 | tf_op jit(solution)/shard_map/while
  82.3 5.8 %collective-permute-start.4 = (bf16[64,256]{1,0:T(8,128)(2,1)S(1)}, bf16[64,256]{1,0:T(8,128)(2,1)S(1)}, u32[]{:S(2)}, u32[]{:S(2)}) collective-permute-start(bf16[64,256]{1,0:T(8,128)(2,1)S(1)} %copy.32), channel_id=1, source_target_pairs={{0,1},{1,2},{2,3},{3,0},{4,5},{5,6},{6,7},{7,4},{8,9},{9,10},{10,1... | collective-permute-start | bytes 98312 | tf_op jit(solution)/shard_map/while/body/eval_jaxpr/ppermute | solution.py:11
  82.4 5.7 %collective-permute-start.5 = (f32[64]{0:T(128)S(1)}, f32[64]{0:T(128)S(1)}, u32[]{:S(2)}, u32[]{:S(2)}) collective-permute-start(f32[64]{0:T(128)S(1)} %copy.33), channel_id=1, source_target_pairs={{0,1},{1,2},{2,3},{3,0},{4,5},{5,6},{6,7},{7,4},{8,9},{9,10},{10,1... | collective-permute-start | bytes 776 | tf_op jit(solution)/shard_map/while/body/eval_jaxpr/ppermute | solution.py:11
  86.1 3.7 %collective-permute-start.6 = (f32[64,256]{1,0:T(8,128)S(1)}, f32[64,256]{1,0:T(8,128)S(1)}, u32[]{:S(2)}, u32[]{:S(2)}) collective-permute-start(f32[64,256]{1,0:T(8,128)S(1)} %fusion.61), channel_id=1, source_target_pairs={{0,1},{1,2},{2,3},{3,0},{4,5},{5,6},{6,7},{7,4},{8,9},{9,10},{10,1... | collective-permute-start | bytes 196616 | tf_op jit(solution)/shard_map/while/body/eval_jaxpr/ppermute | solution.py:11
  89.9 2.6 copy-start.1
  89.9 6.4 %collective-permute-start.4 = (bf16[64,256]{1,0:T(8,128)(2,1)S(1)}, bf16[64,256]{1,0:T(8,128)(2,1)S(1)}, u32[]{:S(2)}, u32[]{:S(2)}) collective-permute-start(bf16[64,256]{1,0:T(8,128)(2,1)S(1)} %copy.32), channel_id=1, source_target_pairs={{0,1},{1,2},{2,3},{3,0},{4,5},{5,6},{6,7},{7,4},{8,9},{9,10},{10,1... | collective-permute-start | bytes 98312 | tf_op jit(solution)/shard_map/while/body/eval_jaxpr/ppermute | solution.py:11
  89.9 6.4 %collective-permute-start.5 = (f32[64]{0:T(128)S(1)}, f32[64]{0:T(128)S(1)}, u32[]{:S(2)}, u32[]{:S(2)}) collective-permute-start(f32[64]{0:T(128)S(1)} %copy.33), channel_id=1, source_target_pairs={{0,1},{1,2},{2,3},{3,0},{4,5},{5,6},{6,7},{7,4},{8,9},{9,10},{10,1... | collective-permute-start | bytes 776 | tf_op jit(solution)/shard_map/while/body/eval_jaxpr/ppermute | solution.py:11
  92.7 3.7 %collective-permute-start.6 = (f32[64,256]{1,0:T(8,128)S(1)}, f32[64,256]{1,0:T(8,128)S(1)}, u32[]{:S(2)}, u32[]{:S(2)}) collective-permute-start(f32[64,256]{1,0:T(8,128)S(1)} %fusion.61), channel_id=1, source_target_pairs={{0,1},{1,2},{2,3},{3,0},{4,5},{5,6},{6,7},{7,4},{8,9},{9,10},{10,1... | collective-permute-start | bytes 196616 | tf_op jit(solution)/shard_map/while/body/eval_jaxpr/ppermute | solution.py:11
  96.5 3.5 %copy-start.1 = (bf16[2048,256]{1,0:T(8,128)(2,1)S(1)}, bf16[2048,256]{1,0:T(8,128)(2,1)}, u32[]{:S(2)}) copy-start(bf16[2048,256]{1,0:T(8,128)(2,1)} %get-tuple-element.868) | copy-start | bytes 3145732 | tf_op jit(solution)/shard_map/while
  96.5 7.7 %collective-permute-start.4 = (bf16[64,256]{1,0:T(8,128)(2,1)S(1)}, bf16[64,256]{1,0:T(8,128)(2,1)S(1)}, u32[]{:S(2)}, u32[]{:S(2)}) collective-permute-start(bf16[64,256]{1,0:T(8,128)(2,1)S(1)} %copy.32), channel_id=1, source_target_pairs={{0,1},{1,2},{2,3},{3,0},{4,5},{5,6},{6,7},{7,4},{8,9},{9,10},{10,1... | collective-permute-start | bytes 98312 | tf_op jit(solution)/shard_map/while/body/eval_jaxpr/ppermute | solution.py:11
  97.8 6.3 %collective-permute-start.5 = (f32[64]{0:T(128)S(1)}, f32[64]{0:T(128)S(1)}, u32[]{:S(2)}, u32[]{:S(2)}) collective-permute-start(f32[64]{0:T(128)S(1)} %copy.33), channel_id=1, source_target_pairs={{0,1},{1,2},{2,3},{3,0},{4,5},{5,6},{6,7},{7,4},{8,9},{9,10},{10,1... | collective-permute-start | bytes 776 | tf_op jit(solution)/shard_map/while/body/eval_jaxpr/ppermute | solution.py:11
  100.3 3.9 %collective-permute-start.6 = (f32[64,256]{1,0:T(8,128)S(1)}, f32[64,256]{1,0:T(8,128)S(1)}, u32[]{:S(2)}, u32[]{:S(2)}) collective-permute-start(f32[64,256]{1,0:T(8,128)S(1)} %fusion.61), channel_id=1, source_target_pairs={{0,1},{1,2},{2,3},{3,0},{4,5},{5,6},{6,7},{7,4},{8,9},{9,10},{10,1... | collective-permute-start | bytes 196616 | tf_op jit(solution)/shard_map/while/body/eval_jaxpr/ppermute | solution.py:11
  104.2 3.5 %copy-start.1 = (bf16[2048,256]{1,0:T(8,128)(2,1)S(1)}, bf16[2048,256]{1,0:T(8,128)(2,1)}, u32[]{:S(2)}) copy-start(bf16[2048,256]{1,0:T(8,128)(2,1)} %get-tuple-element.868) | copy-start | bytes 3145732 | tf_op jit(solution)/shard_map/while
  104.2 7.5 %collective-permute-start.4 = (bf16[64,256]{1,0:T(8,128)(2,1)S(1)}, bf16[64,256]{1,0:T(8,128)(2,1)S(1)}, u32[]{:S(2)}, u32[]{:S(2)}) collective-permute-start(bf16[64,256]{1,0:T(8,128)(2,1)S(1)} %copy.32), channel_id=1, source_target_pairs={{0,1},{1,2},{2,3},{3,0},{4,5},{5,6},{6,7},{7,4},{8,9},{9,10},{10,1... | collective-permute-start | bytes 98312 | tf_op jit(solution)/shard_map/while/body/eval_jaxpr/ppermute | solution.py:11
  104.5 7.2 %collective-permute-start.5 = (f32[64]{0:T(128)S(1)}, f32[64]{0:T(128)S(1)}, u32[]{:S(2)}, u32[]{:S(2)}) collective-permute-start(f32[64]{0:T(128)S(1)} %copy.33), channel_id=1, source_target_pairs={{0,1},{1,2},{2,3},{3,0},{4,5},{5,6},{6,7},{7,4},{8,9},{9,10},{10,1... | collective-permute-start | bytes 776 | tf_op jit(solution)/shard_map/while/body/eval_jaxpr/ppermute | solution.py:11
  108.0 3.7 %collective-permute-start.6 = (f32[64,256]{1,0:T(8,128)S(1)}, f32[64,256]{1,0:T(8,128)S(1)}, u32[]{:S(2)}, u32[]{:S(2)}) collective-permute-start(f32[64,256]{1,0:T(8,128)S(1)} %fusion.61), channel_id=1, source_target_pairs={{0,1},{1,2},{2,3},{3,0},{4,5},{5,6},{6,7},{7,4},{8,9},{9,10},{10,1... | collective-permute-start | bytes 196616 | tf_op jit(solution)/shard_map/while/body/eval_jaxpr/ppermute | solution.py:11
  111.8 66.9 %copy-start.3 = (f32[256,1024]{1,0:T(8,128)S(1)}, f32[256,1024]{1,0:T(8,128)}, u32[]{:S(2)}) copy-start(f32[256,1024]{1,0:T(8,128)} %copy-done.2) | copy-start | bytes 3145732
  111.8 66.9 %copy-start.4 = (bf16[1,256,512]{2,1,0:T(8,128)(2,1)S(1)}, bf16[1,256,512]{2,1,0:T(8,128)(2,1)}, u32[]{:S(2)}) copy-start(bf16[1,256,512]{2,1,0:T(8,128)(2,1)} %param.13) | copy-start | bytes 786436
  111.8 209.8 %all-reduce.3.cloned.1.call-start = ((), (), s32[]{:S(2)}) async-start(), calls=%async_computation.3 | async-start | bytes 6291456 | tf_op jit(solution)/shard_map/psum | solution.py:108
  178.7 3.2 copy-start.7
Sparse Core Ops, SparseCore 0:
  12.0 42.8 all-gather.1
  111.9 66.7 reduce-scatter.1
  184.8 136.6 all-reduce.2
where the time goes:
time: 335 us
  waiting for transfers between devices  258 us (77%)
  matrix products  34.1 us (10%)
  starting transfers between devices  16 us (5%)
  between operations  13.8 us (4%)
  other arithmetic  6.81 us (2%)
  local copies, waits for them, and re-layouts  5.39 us (2%)
    psum x1, waiting for transfers between devices, on_device(): tower_sums = lax.psum((first_term, second_term), ('query', 'item'))  138 us
    reduce_scatter x1, waiting for transfers between devices, on_device(): lax.psum_scatter(emb_grad, 'query', scatter_dimension=0, tiled=True)  66.9 us
    all_gather x1, waiting for transfers between devices, on_device(): item_tile = lax.all_gather(own_emb, 'query', axis=0, tiled=True)  42.9 us
    ppermute x28, starting transfers between devices, passed_along(): return lax.ppermute(x, axis, [(i, (i + by) % count) for i in range(count)])  15.9 us
    dot_general x8, matrix products, tile_scores(): jnp.einsum('qe,ie->qi', queries, item_tile, preferred_element_type=jnp.fl...  13.8 us
    dot_general x4, matrix products, tile_grads(): jnp.einsum('qi,qe->ie', coeffs, queries, preferred_element_type=jnp.float32)  11.9 us
    ppermute x28, waiting for transfers between devices, passed_along(): return lax.ppermute(x, axis, [(i, (i + by) % count) for i in range(count)])  10.1 us
  transfers between devices with their start and end apart: 31, of which 18 were waited for; matrix products, arithmetic and copies ran while one was open for 9% of the time, Pallas kernels for 0%

commit v1 on v0

v1 whole, which is shorter than its diff:
```python
import math

import jax
import jax.numpy as jnp
from jax import lax
from jax.sharding import PartitionSpec as P

BOTH = ("query", "item")


def on_device(query_emb, targets, eligible_tiles, item_feats, w_first, w_second):
    q_rows = query_emb.shape[0]
    item_count = lax.axis_size("item")
    query_count = lax.axis_size("query")
    item_pos = lax.axis_index("item")
    query_pos = lax.axis_index("query")
    tokens = item_feats.reshape(item_feats.shape[1], item_feats.shape[2])
    block_rows = tokens.shape[0]
    queries = lax.all_gather(query_emb, "query", axis=0, tiled=True)
    own_targets = lax.dynamic_slice_in_dim(targets, item_pos * q_rows, q_rows, 0)
    small = jnp.concatenate([eligible_tiles.reshape(-1), own_targets])
    small = lax.all_gather(small, BOTH, axis=0).reshape(query_count, item_count, -1)
    flags = small[:, :, : eligible_tiles.size].reshape((query_count, item_count) + eligible_tiles.shape)
    flags = lax.dynamic_slice(
        flags, (0, 0, item_pos, query_pos), (query_count, item_count, 1, 1)
    ).reshape(query_count, item_count)
    wanted = lax.dynamic_slice_in_dim(small[:, :, eligible_tiles.size :], item_pos, 1, 1).reshape(-1)

    pre_act = jnp.dot(tokens, w_first, preferred_element_type=jnp.float32)
    hidden = jax.nn.silu(pre_act).astype(jnp.bfloat16)
    own_emb = jnp.dot(hidden, w_second, preferred_element_type=jnp.float32).astype(jnp.bfloat16)
    items = lax.all_gather(own_emb, "item", axis=0, tiled=True)
    block_of = jnp.arange(item_count, dtype=jnp.int32) * query_count + query_pos
    item_ids = (
        block_of[:, None] * block_rows + jnp.arange(block_rows, dtype=jnp.int32)[None, :]
    ).reshape(-1)
    live = jnp.broadcast_to(
        flags[:, None, :, None] > 0, (query_count, q_rows, item_count, block_rows)
    ).reshape(query_count * q_rows, item_count * block_rows)
    scores = 0.25 * jnp.einsum("qe,ie->qi", queries, items, preferred_element_type=jnp.float32)
    hit = item_ids[None, :] == wanted[:, None]
    masked = jnp.where(live, scores, -1e30)
    top = jnp.max(masked, axis=1)
    total = jnp.sum(jnp.where(live, jnp.exp(masked - top[:, None]), 0.0), axis=1)
    positive = jnp.sum(jnp.where(hit, scores, 0.0), axis=1)
    stats = lax.all_gather(jnp.stack([top, total, positive]), "query", axis=0)
    all_top = jnp.max(stats[:, 0], axis=0)
    all_total = jnp.sum(stats[:, 1] * jnp.exp(stats[:, 0] - all_top[None]), axis=0)
    log_norm = all_top + jnp.log(all_total)
    loss = lax.dynamic_slice_in_dim(
        log_norm - jnp.sum(stats[:, 2], axis=0), query_pos * q_rows, q_rows, 0
    )
    weights = jnp.where(live, jnp.exp(masked - log_norm[:, None]), 0.0)
    coeffs = (weights - hit.astype(jnp.float32)).astype(jnp.bfloat16)
    e_part = 0.25 * jnp.einsum("qi,qe->ie", coeffs, queries, preferred_element_type=jnp.float32)
    own_grad = lax.psum_scatter(e_part, "item", scatter_dimension=0, tiled=True).astype(
        jnp.bfloat16
    )
    q_part = 0.25 * jnp.dot(coeffs, items, preferred_element_type=jnp.float32)
    query_grad = lax.psum_scatter(q_part, "query", scatter_dimension=0, tiled=True)
    second_term = jnp.einsum("ih,ie->he", hidden, own_grad, preferred_element_type=jnp.float32)
    hid_grad = jnp.einsum("ie,he->ih", own_grad, w_second, preferred_element_type=jnp.float32)
    gate_sig = jax.nn.sigmoid(pre_act)
    pre_grad = (hid_grad * gate_sig * (1.0 + pre_act * (1.0 - gate_sig))).astype(jnp.bfloat16)
    first_term = jnp.einsum("id,ih->dh", tokens, pre_grad, preferred_element_type=jnp.float32)
    tower_sums = lax.psum((first_term, second_term), BOTH)
    grad_scale = 1.0 / math.sqrt(block_rows * query_count * item_count)
    return (loss, query_grad, tower_sums[0] * grad_scale, tower_sums[1] * grad_scale)


def solution(mesh):
    return jax.shard_map(
        on_device,
        mesh=mesh,
        in_specs=(
            P(("query", "item"), None),
            P("query"),
            P("query", "item"),
            P("item", "query", None),
            P(),
            P(),
        ),
        out_specs=(P(("query", "item")), P(("query", "item"), None), P(), P()),
        check_vma=False,
    )
```

time: 335 us -> 311 us (0.928)
  blocking collectives: 0 us -> 112 us
  waiting for transfers between devices: 258 us -> 161 us
  matrix products: 34.1 us -> 10.3 us
  starting transfers between devices: 16 us -> 0.12 us
    all_gather x0 -> x3, blocking collectives: none -> 69.5 us  [the longest x1 31 us: on_device(): queries = lax.all_gather(query_emb, 'query', axis=0, tiled=True)]
    reduce_scatter x1 -> x2, waiting for transfers between devices: 66.9 us -> 23.9 us  [the longest x1 23.9 us: on_device(): lax.psum_scatter(e_part, 'item', scatter_dimension=0, tiled=True)]
    all_gather x1 -> x0, waiting for transfers between devices: 42.9 us -> none  [on_device(): item_tile = lax.all_gather(own_emb, 'query', axis=0, tiled=True)]
    unnamed x0 -> x1, blocking collectives: none -> 42.1 us
    dot_general x16 -> x3, matrix products: 26.9 us -> 3.22 us  [the longest x1 1.4 us: on_device(): jnp.einsum('qi,qe->ie', coeffs, queries, preferred_element_type=jnp.float32)]
    ppermute x28 -> x0, starting transfers between devices: 15.9 us -> none  [passed_along(): return lax.ppermute(x, axis, [(i, (i + by) % count) for i in range(count)])]
    ppermute x28 -> x0, waiting for transfers between devices: 10.1 us -> none  [passed_along(): return lax.ppermute(x, axis, [(i, (i + by) % count) for i in range(count)])]
  transfers between devices with their start and end apart: 31 -> 3, of which waited for: 18 -> 2; matrix products, arithmetic and copies ran while one was open for 9% -> 3% of each run, Pallas kernels for 0% -> 0%
where the time goes in v1:
time: 311 us
  waiting for transfers between devices  161 us (52%)
  blocking collectives  112 us (36%)
  between operations  15.7 us (5%)
  matrix products  10.3 us (3%)
  local copies, waits for them, and re-layouts  6.23 us (2%)
  other arithmetic  6.14 us (2%)
    psum x1, waiting for transfers between devices, on_device(): tower_sums = lax.psum((first_term, second_term), BOTH)  137 us
    unnamed x1, blocking collectives  42.1 us
    all_gather x1, blocking collectives, on_device(): queries = lax.all_gather(query_emb, 'query', axis=0, tiled=True)  31 us
    all_gather x1, blocking collectives, on_device(): stats = lax.all_gather(jnp.stack([top, total, positive]), 'query', axis=0)  30.5 us
    reduce_scatter x1, waiting for transfers between devices, on_device(): lax.psum_scatter(e_part, 'item', scatter_dimension=0, tiled=True)  23.9 us
    all_gather x1, blocking collectives, on_device(): items = lax.all_gather(own_emb, 'item', axis=0, tiled=True)  8.01 us
  transfers between devices with their start and end apart: 3, of which 2 were waited for; matrix products, arithmetic and copies ran while one was open for 3% of the time, Pallas kernels for 0%

profile of v1, /device:TPU:0, one launch (start us, length us, event | category | flops | bytes accessed | tf_op | source)
XLA Modules:
  0.0 311.0 jit_solution(3521980565822129825)
XLA Ops:
  8.0 0.0 copy-start
  8.0 0.0 copy-start.2
  8.0 0.0 reduce-scatter.5.cloned.1.call-start
  8.1 0.9 reshape.62
  8.9 0.1 add_bitcast_fusion
  9.0 0.8 dynamic_slice.12
  9.8 0.2 add_dynamic-update-slice_fusion
  9.9 42.1 %all-reduce = s32[3072]{0:T(1024)S(1)} all-reduce(s32[3072]{0:T(1024)S(1)} %add_dynamic-update-slice_fusion), channel_id=2, replica_groups=mesh['query'=8,'item'=4] {'query','item'}, use_global_device_ids=true, to_apply=%add | all-reduce | flops 3072 | bytes 24576
  52.1 0.1 reshape.63
  52.1 0.1 slice.22
  52.2 0.1 eq.16
  52.3 0.1 copy.26
  52.4 0.1 copy.20
  52.5 31.0 %all_gather.21 = bf16[512,256]{1,0:T(8,128)(2,1)S(1)} all-gather(bf16[64,256]{1,0:T(8,128)(2,1)} %param.6), channel_id=1, replica_groups=mesh['query'=8,'item'=4] {'query'}, dimensions={0}, use_global_device_ids=true | all-gather | bytes 294912 | tf_op jit(solution)/shard_map/all_gather | solution.py:19
  83.5 0.3 broadcast_in_dim.19
  83.9 0.0 copy-start.3
  83.9 0.3 copy.30
  84.2 0.6 copy.21
  84.8 0.0 copy-done
  84.8 0.0 copy-done.2
  84.8 0.4 fusion.11
  85.2 0.0 copy-done.3
  85.3 0.0 copy-start.1
  85.3 0.4 convolution_convert_fusion
  85.7 0.5 copy-done.1
  86.2 8.0 %all_gather.20 = bf16[1024,256]{1,0:T(8,128)(2,1)S(1)} all-gather(bf16[256,256]{1,0:T(8,128)(2,1)S(1)} %convolution_convert_fusion), channel_id=1, replica_groups=mesh['query'=8,'item'=4] {'item'}, dimensions={0}, use_global_device_ids=true | all-gather | bytes 655360 | tf_op jit(solution)/shard_map/all_gather | solution.py:32
  94.2 0.6 fusion.3
  94.8 0.8 select_reduce_fusion
  95.7 30.5 %all-gather.2 = f32[8,3,512]{2,1,0:T(4,128)S(1)} all-gather(f32[1,3,512]{2,1,0:T(4,128)S(1)} %maximum_bitcast_fusion), channel_id=3, replica_groups=mesh['query'=8,'item'=4] {'query'}, dimensions={0}, use_global_device_ids=true | all-gather | bytes 55296 | tf_op jit(solution)/shard_map/all_gather | solution.py:46
  126.2 0.1 fusion.24
  126.3 0.8 fusion.2
  127.1 1.4 convolution_multiply_fusion.1
  128.5 0.0 reduce-scatter.5.cloned.1.call-update
  128.5 0.0 all-reduce.4.cloned.1.call-start
  128.6 23.9 %reduce-scatter.5.cloned.1.call-done = f32[256,256]{1,0:T(8,128)} async-done(((f32[1024,256]{1,0:T(8,128)}), f32[256,256]{1,0:T(8,128)}) %reduce-scatter.5.cloned.1.call-update) | async-done | bytes 262160 | tf_op jit(solution)/shard_map/reduce_scatter | solution.py:56
  152.4 2.8 fusion.13
  155.2 3.4 %convolution_bitcast_fusion = f32[512,1024]{0,1:T(8,128)} fusion(bf16[1024,256]{1,0:T(8,128)(2,1)S(1)} %copy-done.3, f32[256,1024]{1,0:T(8,128)} %copy-done.1, bf16[1,256,512]{2,1,0:T(8,128)(2,1)S(1)} %copy-done.2, f32[256,256]{1,0:T(8,128)} %reduce-scatter.5.cloned.1.call-done), kind=kOutput, calls=%fused_computation.7 | convolution fusion | flops 405078016 | bytes 4194304 | tf_op jit(solution)/shard_map/id,ih->dh/dot_general | solution.py:65
  158.7 0.0 all-reduce.4.cloned.1.call-update
  158.7 0.0 reduce-scatter.3.cloned.1.call-start
  158.8 1.3 convolution_multiply_fusion.2
  160.0 0.0 reduce-scatter.3.cloned.1.call-update
  160.1 0.6 dynamic_slice.15
  160.6 136.9 %all-reduce.4.cloned.1.call-done = (f32[512,1024]{0,1:T(8,128)}, f32[1024,256]{1,0:T(8,128)}) async-done(((f32[512,1024]{0,1:T(8,128)}, f32[1024,256]{1,0:T(8,128)}), (f32[512,1024]{0,1:T(8,128)}, f32[1024,256]{1,0:T(8,128)})) %all-reduce.4.cloned.1.call-update) | async-done | bytes 3145744 | tf_op jit(solution)/shard_map/psum | solution.py:66
  297.6 1.8 broadcast_multiply_fusion
  299.4 1.8 copy.25
  301.2 2.3 broadcast_multiply_fusion.1
  303.5 0.0 reduce-scatter.3.cloned.1.call-done
  (8 shorter events, 0.1 us)
Async XLA Ops:
  8.0 76.8 %copy-start = (bf16[512,1024]{1,0:T(8,128)(2,1)S(1)}, bf16[512,1024]{1,0:T(8,128)(2,1)}, u32[]{:S(2)}) copy-start(bf16[512,1024]{1,0:T(8,128)(2,1)} %param.10) | copy-start | bytes 3145732
  8.0 76.8 %copy-start.2 = (bf16[1,256,512]{2,1,0:T(8,128)(2,1)S(1)}, bf16[1,256,512]{2,1,0:T(8,128)(2,1)}, u32[]{:S(2)}) copy-start(bf16[1,256,512]{2,1,0:T(8,128)(2,1)} %param.9) | copy-start | bytes 786436
  8.0 144.4 %reduce-scatter.5.cloned.1.call-start = ((), (), s32[]{:S(2)}) async-start(), calls=%async_computation.3 | async-start | bytes 1310720 | tf_op jit(solution)/shard_map/reduce_scatter | solution.py:56
  83.9 1.4 copy-start.3
  85.3 1.0 copy-start.1
  128.5 169.1 %all-reduce.4.cloned.1.call-start = ((), (), s32[]{:S(2)}) async-start(), calls=%async_computation.4 | async-start | bytes 6291456 | tf_op jit(solution)/shard_map/psum | solution.py:66
  158.7 144.8 %reduce-scatter.3.cloned.1.call-start = ((), (), s32[]{:S(2)}) async-start(), calls=%async_computation.2 | async-start | bytes 589824 | tf_op jit(solution)/shard_map/reduce_scatter | solution.py:60
Sparse Core Ops, SparseCore 0:
  128.6 23.7 reduce-scatter.4
  158.8 138.7 all-reduce.3
Sparse Core Ops, SparseCore 1:
  163.1 62.8 reduce-scatter.2

commit v2 on v1

v2 whole, which is shorter than its diff:
```python
import functools
import math

import jax
import jax.numpy as jnp
from jax import lax
from jax.experimental import pallas as pl
from jax.experimental.pallas import tpu as pltpu
from jax.sharding import PartitionSpec as P

F32 = jnp.float32
BF16 = jnp.bfloat16


def dot(a, b, contract):
    return lax.dot_general(a, b, ((contract[:1], contract[1:]), ((), ())), preferred_element_type=F32)


def rows(start, size):
    return pl.ds(pl.multiple_of(start, math.gcd(size, 256)), size)


def window_kernel(
    shape,
    query_ref, meta_ref, tokens_ref, w1_ref, w2_ref,
    loss_ref, qgrad_ref, g1_ref, g2_ref,
    q_all, meta_in, emb_all, flags_all, scores, coeffs, stats_all,
    e_acc, e_recv_c, e_recv_x, q_acc, q_recv_y, q_recv_z,
    pre_act, hidden,
    a_acc, a_recv_c, a_recv_x, a_recv_y, a_recv_z, a_out,
    b_acc, b_recv_c, b_recv_x, b_recv_y, b_recv_z, b_out,
    send_sems, recv_sems,
):
    nq, ni, grad_scale = shape
    gx, gz = ni // 2, nq // 2
    q, i = lax.axis_index("query"), lax.axis_index("item")
    core, x = lax.rem(i, 2), lax.div(i, 2)
    y, z = lax.rem(q, 2), lax.div(q, 2)
    q_rows, width = query_ref.shape
    n_q = nq * q_rows
    block = tokens_ref.shape[0]
    used = [0]

    def send(src, dst, peer):
        slot = used[0]
        used[0] += 1
        copy = pltpu.make_async_remote_copy(
            src_ref=src, dst_ref=dst, send_sem=send_sems.at[slot], recv_sem=recv_sems.at[slot],
            device_id=peer, device_id_type=pl.DeviceIdType.MESH,
        )
        copy.start()
        return copy

    def finish(copies):
        for copy in copies:
            copy.wait()

    axes = {
        "core": (2, core, lambda t: {"item": x * 2 + t}),
        "x": (gx, x, lambda t: {"item": t * 2 + core}),
        "y": (2, y, lambda t: {"query": z * 2 + t}),
        "z": (gz, z, lambda t: {"query": t * 2 + y}),
    }

    def reduce_start(acc, recv, base, size, axis):
        group, own, peer = axes[axis]
        copies = []
        for k in range(1, group):
            there = lax.rem(own + k, group)
            copies.append(
                send(acc.at[rows(base + there * size, size)], recv.at[rows((k - 1) * size, size)], peer(there))
            )
        return copies

    def reduce_finish(copies, acc, recv, base, size, axis):
        group, own, _ = axes[axis]
        finish(copies)
        here = rows(base + own * size, size)
        total = acc[here, :]
        for k in range(1, group):
            total = total + recv[rows((k - 1) * size, size), :]
        acc[here, :] = total
        return base + own * size

    def gather_start(buf, base, size, axis):
        group, own, peer = axes[axis]
        here = buf.at[rows(base + own * size, size)]
        return [send(here, here, peer(lax.rem(own + k, group))) for k in range(1, group)]

    barrier = pltpu.get_barrier_semaphore()
    for k in range(1, nq):
        pl.semaphore_signal(
            barrier, inc=1, device_id={"query": lax.rem(q + k, nq)}, device_id_type=pl.DeviceIdType.MESH
        )
    for k in range(1, ni):
        pl.semaphore_signal(
            barrier, inc=1, device_id={"item": lax.rem(i + k, ni)}, device_id_type=pl.DeviceIdType.MESH
        )
    pl.semaphore_wait(barrier, nq + ni - 2)

    q_pos = y * gz + z
    copies = []
    for k in range(1, nq):
        there = lax.rem(q + k, nq)
        copies.append(send(meta_ref.at[there], meta_in.at[k], {"query": there}))
        copies.append(send(query_ref, q_all.at[rows(q_pos * q_rows, q_rows)], {"query": there}))
    q_all[rows(q_pos * q_rows, q_rows), :] = query_ref[...]
    meta_in[0] = meta_ref[q]

    tokens = tokens_ref[...]
    pre = dot(tokens, w1_ref[...], (1, 0))
    pre_act[...] = pre
    hidden[...] = jax.nn.silu(pre).astype(BF16)
    i_pos = core * gx + x
    emb_all[rows(i_pos * block, block), :] = dot(hidden[...], w2_ref[...], (1, 0)).astype(BF16)

    finish(copies)
    flags = meta_in[0]
    for k in range(1, nq):
        flags = flags + meta_in[k]
    meta_rows = flags.shape[0]
    flags_all[rows(i_pos * meta_rows, meta_rows), :] = flags
    wanted = flags[ni : ni + 1, :]

    finish(
        gather_start(emb_all, core * gx * block, block, "x")
        + gather_start(flags_all, core * gx * meta_rows, meta_rows, "x")
    )
    finish(
        gather_start(emb_all, 0, gx * block, "core") + gather_start(flags_all, 0, gx * meta_rows, "core")
    )

    def located(p):
        item = lax.rem(p, gx) * 2 + lax.div(p, gx)
        first = (item * nq + q) * block
        ids = lax.broadcasted_iota(jnp.int32, (block, n_q), 0)
        hit = ids == (wanted - first)
        live = flags_all[pl.ds(p * meta_rows + i, 1), :] > 0
        return hit, live

    def score_block(p, carried):
        top, total, positive = carried
        hit, live = located(p)
        s = 0.25 * dot(emb_all[rows(p * block, block), :], q_all[...], (1, 1))
        scores[rows(p * block, block), :] = s
        here = jnp.max(s, axis=0, keepdims=True)
        added = jnp.sum(jnp.exp(s - here), axis=0, keepdims=True)
        positive = positive + jnp.sum(jnp.where(hit, s, 0.0), axis=0, keepdims=True)
        here = jnp.where(live, here, -1e30)
        new_top = jnp.maximum(top, here)
        total = total * jnp.exp(top - new_top) + jnp.where(live, added * jnp.exp(here - new_top), 0.0)
        return new_top, total, positive

    start = (jnp.full((1, n_q), -1e30, F32), jnp.zeros((1, n_q), F32), jnp.zeros((1, n_q), F32))
    top, total, positive = lax.fori_loop(0, ni, score_block, start)
    stats_all[0] = jnp.concatenate([top, total, positive, jnp.zeros((5, n_q), F32)], axis=0)
    finish([
        send(stats_all.at[0], stats_all.at[k], {"query": lax.rem(q + k, nq)}) for k in range(1, nq)
    ])
    top = stats_all[0, 0:1, :]
    for k in range(1, nq):
        top = jnp.maximum(top, stats_all[k, 0:1, :])
    total = jnp.zeros((1, n_q), F32)
    positive = jnp.zeros((1, n_q), F32)
    for k in range(nq):
        total = total + stats_all[k, 1:2, :] * jnp.exp(stats_all[k, 0:1, :] - top)
        positive = positive + stats_all[k, 2:3, :]
    log_norm = top + jnp.log(total)
    loss_ref[...] = log_norm - positive

    def grad_block(p, carried):
        hit, live = located(p)
        s = scores[rows(p * block, block), :]
        weights = jnp.where(live, jnp.exp(s - log_norm), 0.0)
        c = (weights - hit.astype(F32)).astype(BF16)
        coeffs[rows(p * block, block), :] = c
        e_acc[rows(p * block, block), :] = 0.25 * dot(c, q_all[...], (1, 0))
        return carried

    lax.fori_loop(0, ni, grad_block, 0)
    e_copies = reduce_start(e_acc, e_recv_c, 0, gx * block, "core")
    q_acc[...] = 0.25 * dot(coeffs[...], emb_all[...], (0, 0))
    q_copies = reduce_start(q_acc, q_recv_y, 0, gz * q_rows, "y")
    e_base = reduce_finish(e_copies, e_acc, e_recv_c, 0, gx * block, "core")
    e_copies = reduce_start(e_acc, e_recv_x, e_base, block, "x")
    e_base = reduce_finish(e_copies, e_acc, e_recv_x, e_base, block, "x")
    own_grad = e_acc[rows(e_base, block), :].astype(BF16)

    second = dot(hidden[...], own_grad, (0, 0))
    hid = second.shape[0]
    b_rows, a_rows = b_acc.shape[0], a_acc.shape[0]
    din = tokens.shape[1]
    for j in range(width // 128):
        b_acc[j * hid : (j + 1) * hid, :] = second[:, j * 128 : (j + 1) * 128]
    b_size = b_rows // 2
    b_copies = reduce_start(b_acc, b_recv_c, 0, b_size, "core")
    hid_grad = dot(own_grad, w2_ref[...], (1, 1))
    pre = pre_act[...]
    sig = jax.nn.sigmoid(pre)
    pre_grad = (hid_grad * sig * (1.0 + pre * (1.0 - sig))).astype(BF16)
    first = dot(tokens, pre_grad, (0, 0))
    for j in range(hid // 128):
        a_acc[j * din : (j + 1) * din, :] = first[:, j * 128 : (j + 1) * 128]
    a_size = a_rows // 2
    a_copies = reduce_start(a_acc, a_recv_c, 0, a_size, "core")

    q_base = reduce_finish(q_copies, q_acc, q_recv_y, 0, gz * q_rows, "y")
    b_base = reduce_finish(b_copies, b_acc, b_recv_c, 0, b_size, "core")
    b_size = b_size // 2
    b_copies = reduce_start(b_acc, b_recv_y, b_base, b_size, "y")
    a_base = reduce_finish(a_copies, a_acc, a_recv_c, 0, a_size, "core")
    a_size = a_size // gx
    a_copies = reduce_start(a_acc, a_recv_x, a_base, a_size, "x")
    q_copies = reduce_start(q_acc, q_recv_z, q_base, q_rows, "z")
    b_base = reduce_finish(b_copies, b_acc, b_recv_y, b_base, b_size, "y")
    b_size = b_size // gx
    b_copies = reduce_start(b_acc, b_recv_x, b_base, b_size, "x")
    q_base = reduce_finish(q_copies, q_acc, q_recv_z, q_base, q_rows, "z")
    qgrad_ref[...] = q_acc[rows(q_base, q_rows), :]
    a_base = reduce_finish(a_copies, a_acc, a_recv_x, a_base, a_size, "x")
    a_size = a_size // 2
    a_copies = reduce_start(a_acc, a_recv_y, a_base, a_size, "y")
    b_base = reduce_finish(b_copies, b_acc, b_recv_x, b_base, b_size, "x")
    b_size = b_size // gz
    b_copies = reduce_start(b_acc, b_recv_z, b_base, b_size, "z")
    a_base = reduce_finish(a_copies, a_acc, a_recv_y, a_base, a_size, "y")
    a_size = a_size // gz
    a_copies = reduce_start(a_acc, a_recv_z, a_base, a_size, "z")

    b_base = reduce_finish(b_copies, b_acc, b_recv_z, b_base, b_size, "z")
    b_out[rows(b_base, b_size), :] = (b_acc[rows(b_base, b_size), :] * grad_scale).astype(b_out.dtype)
    b_base = b_base - z * b_size
    b_copies = gather_start(b_out, b_base, b_size, "z")
    a_base = reduce_finish(a_copies, a_acc, a_recv_z, a_base, a_size, "z")
    a_out[rows(a_base, a_size), :] = (a_acc[rows(a_base, a_size), :] * grad_scale).astype(a_out.dtype)
    a_base = a_base - z * a_size
    a_copies = gather_start(a_out, a_base, a_size, "z")
    finish(b_copies)
    b_size = b_size * gz
    b_base = b_base - x * b_size
    b_copies = gather_start(b_out, b_base, b_size, "x")
    finish(a_copies)
    a_size = a_size * gz
    a_base = a_base - y * a_size
    a_copies = gather_start(a_out, a_base, a_size, "y")
    finish(b_copies)
    b_size = b_size * gx
    b_base = b_base - y * b_size
    b_copies = gather_start(b_out, b_base, b_size, "y")
    finish(a_copies)
    a_size = a_size * 2
    a_base = a_base - x * a_size
    a_copies = gather_start(a_out, a_base, a_size, "x")
    finish(b_copies)
    b_copies = gather_start(b_out, 0, b_rows // 2, "core")
    finish(b_copies)
    for j in range(width // 128):
        g2_ref[:, j * 128 : (j + 1) * 128] = b_out[j * hid : (j + 1) * hid, :].astype(F32)
    finish(a_copies)
    a_copies = gather_start(a_out, 0, a_rows // 2, "core")
    finish(a_copies)
    for j in range(hid // 128):
        g1_ref[:, j * 128 : (j + 1) * 128] = a_out[j * din : (j + 1) * din, :].astype(F32)


def on_device(query_emb, targets, eligible_tiles, item_feats, w_first, w_second):
    q_rows, width = query_emb.shape
    ni, nq = lax.axis_size("item"), lax.axis_size("query")
    gx, gz = ni // 2, nq // 2
    i, q = lax.axis_index("item"), lax.axis_index("query")
    tokens = item_feats.reshape(item_feats.shape[1], item_feats.shape[2])
    block, din = tokens.shape
    hid = w_first.shape[1]
    n_q = nq * q_rows
    q_pos = (q % 2) * gz + q // 2
    meta_rows = -(-(ni + 1) // 8) * 8
    own = lax.dynamic_slice_in_dim(targets, i * q_rows, q_rows, 0)
    flags = jnp.broadcast_to((eligible_tiles > 0).astype(jnp.int32).T[:, :, None], (nq, ni, n_q))
    mine = (jnp.arange(n_q, dtype=jnp.int32) // q_rows == q_pos).astype(jnp.int32)
    meta = jnp.concatenate(
        [
            flags,
            jnp.broadcast_to(jnp.tile(own, nq)[None, None, :], (nq, 1, n_q)),
            jnp.zeros((nq, meta_rows - ni - 1, n_q), jnp.int32),
        ],
        axis=1,
    ) * mine[None, None, :]

    a_rows, b_rows = din * hid // 128, hid * width // 128
    a_dtype = BF16 if a_rows // (nq * ni) % 16 == 0 else F32
    b_dtype = BF16 if b_rows // (nq * ni) % 16 == 0 else F32
    n_copies = 2 * (nq - 1) + 2 * gx + nq - 1 + gx + gz + 4 * (2 + gx - 1 + gz - 1) + 8
    vmem = pltpu.VMEM
    loss, query_grad, g1, g2 = pl.pallas_call(
        functools.partial(window_kernel, (nq, ni, 1.0 / math.sqrt(block * nq * ni))),
        out_shape=(
            jax.ShapeDtypeStruct((1, n_q), F32),
            jax.ShapeDtypeStruct((q_rows, width), F32),
            jax.ShapeDtypeStruct((din, hid), F32),
            jax.ShapeDtypeStruct((hid, width), F32),
        ),
        in_specs=[pl.BlockSpec(memory_space=vmem)] * 5,
        out_specs=(pl.BlockSpec(memory_space=vmem),) * 4,
        scratch_shapes=[
            vmem((n_q, width), BF16),
            vmem((nq, meta_rows, n_q), jnp.int32),
            vmem((ni * block, width), BF16),
            vmem((ni * meta_rows, n_q), jnp.int32),
            vmem((ni * block, n_q), F32),
            vmem((ni * block, n_q), BF16),
            vmem((nq, 8, n_q), F32),
            vmem((ni * block, width), F32),
            vmem((gx * block, width), F32),
            vmem((max(gx - 1, 1) * block, width), F32),
            vmem((n_q, width), F32),
            vmem((gz * q_rows, width), F32),
            vmem((max(gz - 1, 1) * q_rows, width), F32),
            vmem((block, hid), F32),
            vmem((block, hid), BF16),
            vmem((a_rows, 128), F32),
            vmem((a_rows // 2, 128), F32),
            vmem((a_rows // 2 // gx * (gx - 1), 128), F32),
            vmem((a_rows // 4 // gx, 128), F32),
            vmem((a_rows // 4 // gx // gz * (gz - 1), 128), F32),
            vmem((a_rows, 128), a_dtype),
            vmem((b_rows, 128), F32),
            vmem((b_rows // 2, 128), F32),
            vmem((b_rows // 4 // gx * (gx - 1), 128), F32),
            vmem((b_rows // 4, 128), F32),
            vmem((b_rows // 4 // gx // gz * (gz - 1), 128), F32),
            vmem((b_rows, 128), b_dtype),
            pltpu.SemaphoreType.DMA((n_copies,)),
            pltpu.SemaphoreType.DMA((n_copies,)),
        ],
        compiler_params=pltpu.CompilerParams(
            collective_id=0, has_side_effects=True, vmem_limit_bytes=58 * 2**20
        ),
        name="loss_window",
    )(query_emb, meta, tokens, w_first, w_second)
    loss = lax.dynamic_slice_in_dim(loss.reshape(n_q), q_pos * q_rows, q_rows, 0)
    return (loss, query_grad, g1, g2)


def solution(mesh):
    return jax.shard_map(
        on_device,
        mesh=mesh,
        in_specs=(
            P(("query", "item"), None),
            P("query"),
            P("query", "item"),
            P("item", "query", None),
            P(),
            P(),
        ),
        out_specs=(P(("query", "item")), P(("query", "item"), None), P(), P()),
        check_vma=False,
    )
```

time: 311 us -> 101 us (0.32)
  waiting for transfers between devices: 161 us -> 0 us
  blocking collectives: 112 us -> 0 us
  Pallas kernels: 0 us -> 90.6 us
  between operations: 15.7 us -> 0.67 us
  matrix products: 10.3 us -> 0 us
  other arithmetic: 6.14 us -> 1.43 us
    psum x1 -> x0, waiting for transfers between devices: 137 us -> none  [on_device(): tower_sums = lax.psum((first_term, second_term), BOTH)]
    pallas_call x0 -> x1, Pallas kernels: none -> 90.6 us  [on_device(): pl.pallas_call(functools.partial(window_kernel, (nq, ni, 1.0 / math.sqrt(...]
    all_gather x3 -> x0, blocking collectives: 69.5 us -> none  [the longest x1 31 us: on_device(): queries = lax.all_gather(query_emb, 'query', axis=0, tiled=True)]
    unnamed x1 -> x0, blocking collectives: 42.1 us -> none
    reduce_scatter x2 -> x0, waiting for transfers between devices: 23.9 us -> none  [the longest x1 23.9 us: on_device(): lax.psum_scatter(e_part, 'item', scatter_dimension=0, tiled=True)]
    dot_general x7 -> x0, matrix products: 10.3 us -> none  [the longest x1 3.45 us: on_device(): jnp.einsum('id,ih->dh', tokens, pre_grad, preferred_element_type=jnp.floa...]
    mul x3 -> x1, other arithmetic: 4.13 us -> 0.74 us  [on_device(): jnp.concatenate([flags, jnp.broadcast_to(jnp.tile(own, nq)[None, None, :]...]
  transfers between devices with their start and end apart: 3 -> 0, of which waited for: 2 -> 0; matrix products, arithmetic and copies ran while one was open for 3% -> 0% of each run, Pallas kernels for 0% -> 0%
where the time goes in v2:
time: 101 us
  Pallas kernels  90.6 us (90%)
  local copies, waits for them, and re-layouts  8.04 us (8%)
  other arithmetic  1.43 us (1%)
    pallas_call x1, Pallas kernels, on_device(): pl.pallas_call(functools.partial(window_kernel, (nq, ni, 1.0 / math.sqrt(...  90.6 us
    unnamed x5, local copies, waits for them, and re-layouts  5.69 us

profile of v2, /device:TPU:0, one launch (start us, length us, event | category | flops | bytes accessed | tf_op | source)
XLA Modules:
  0.0 100.7 jit_solution(2921574890404515999)
XLA Ops:
  0.7 0.8 dynamic_slice.8
  1.4 0.1 pad.2.clone
  1.5 0.7 convert_bitcast_fusion
  2.2 0.1 copy.10
  2.3 0.1 broadcast_in_dim.18
  2.4 0.1 broadcast_in_dim.8
  2.4 0.7 add_multiply_fusion.meta_ref
  3.2 90.6 %loss_window.1 = (f32[1,512]{1,0:T(1,128)}, f32[64,256]{1,0:T(8,128)}, f32[512,1024]{1,0:T(8,128)}, f32[1024,256]{1,0:T(8,128)}) custom-call(bf16[64,256]{1,0:T(8,128)(2,1)} %query_ref.1, s32[8,8,512]{2,1,0:T(8,128)} %add_multiply_fusion.meta_ref, bf16[256,512]{1,0:T(8,128)(2,1)} %bitcast.5, bf16[512,1024]{1,0:T(8,128)(2,1)} %w1_ref.1, bf16[1024,256]{1,0:T(8,128)(2,1)} %w2_ref.1), custom_call_target="tpu_custom_call" | custom-call | tf_op jit(solution)/shard_map/loss_window/pallas_call | solution.py:294
  93.8 1.3 %dynamic-slice_bitcast_fusion = f32[64]{0:T(128)} fusion(f32[1,512]{1,0:T(1,128)} %get-tuple-element.8, s32[]{:T(128)S(6)} %select_n.30), kind=kLoop, calls=%fused_computation.11 | loop fusion | bytes 516 | tf_op jit(solution)/shard_map/dynamic_slice | solution.py:340
  95.0 1.5 %copy.14 = f32[64,256]{1,0:T(8,128)} copy(f32[64,256]{1,0:T(8,128)} %get-tuple-element.17) | data formatting | bytes 131072
  96.5 0.0 copy-start
  96.5 3.2 %copy.15 = f32[512,1024]{1,0:T(8,128)} copy(f32[512,1024]{1,0:T(8,128)} %get-tuple-element.18) | data formatting | bytes 4194304
  99.8 0.0 copy-done
  99.8 1.0 copy.16
  (4 shorter events, 0.0 us)
Async XLA Ops:
  96.5 3.3 %copy-start = (f32[1024,256]{1,0:T(8,128)S(1)}, f32[1024,256]{1,0:T(8,128)}, u32[]{:S(2)}) copy-start(f32[1024,256]{1,0:T(8,128)} %get-tuple-element.19) | copy-start | bytes 3145732

commit v3 on v2

v3 whole, which is shorter than its diff:
```python
import functools
import math

import jax
import jax.numpy as jnp
from jax import lax
from jax.experimental import pallas as pl
from jax.experimental.pallas import tpu as pltpu
from jax.sharding import PartitionSpec as P

F32 = jnp.float32
BF16 = jnp.bfloat16


def dot(a, b, contract):
    return lax.dot_general(a, b, ((contract[:1], contract[1:]), ((), ())), preferred_element_type=F32)


def rows(start, size):
    return pl.ds(pl.multiple_of(start, math.gcd(size, 256)), size)


def window_kernel(
    shape,
    query_ref, raw_ref, tokens_ref, w1_ref, w2_ref,
    loss_ref, qgrad_ref, a_out, b_out,
    q_all, raw_in, meta_in, emb_all, flags_all, scores, coeffs, stats_all,
    e_acc, e_recv_c, e_recv_x, q_acc, q_recv_y, q_recv_z,
    pre_act, hidden, a_acc, b_acc, core_recv, x_recv, y_recv, z_recv,
    send_sems, recv_sems,
):
    nq, ni, grad_scale = shape
    gx, gz = ni // 2, nq // 2
    q, i = lax.axis_index("query"), lax.axis_index("item")
    core, x = lax.rem(i, 2), lax.div(i, 2)
    y, z = lax.rem(q, 2), lax.div(q, 2)
    q_rows, width = query_ref.shape
    n_q = nq * q_rows
    block = tokens_ref.shape[0]
    used = [0]

    def send(src, dst, peer):
        slot = used[0]
        used[0] += 1
        copy = pltpu.make_async_remote_copy(
            src_ref=src, dst_ref=dst, send_sem=send_sems.at[slot], recv_sem=recv_sems.at[slot],
            device_id=peer, device_id_type=pl.DeviceIdType.MESH,
        )
        copy.start()
        return copy

    def finish(copies):
        for copy in copies:
            copy.wait()

    axes = {
        "core": (2, core, lambda t: {"item": x * 2 + t}),
        "x": (gx, x, lambda t: {"item": t * 2 + core}),
        "y": (2, y, lambda t: {"query": z * 2 + t}),
        "z": (gz, z, lambda t: {"query": t * 2 + y}),
    }

    def reduce_start(acc, recv, base, size, axis):
        group, own, peer = axes[axis]
        copies = []
        for k in range(1, group):
            there = lax.rem(own + k, group)
            copies.append(
                send(acc.at[rows(base + there * size, size)], recv.at[rows((k - 1) * size, size)], peer(there))
            )
        return copies

    def reduce_finish(copies, acc, recv, base, size, axis):
        group, own, _ = axes[axis]
        finish(copies)
        here = rows(base + own * size, size)
        total = acc[here, :]
        for k in range(1, group):
            total = total + recv[rows((k - 1) * size, size), :]
        acc[here, :] = total
        return base + own * size

    def gather_start(buf, base, size, axis):
        group, own, peer = axes[axis]
        here = buf.at[rows(base + own * size, size)]
        return [send(here, here, peer(lax.rem(own + k, group))) for k in range(1, group)]

    barrier = pltpu.get_barrier_semaphore()
    for k in range(1, nq):
        pl.semaphore_signal(
            barrier, inc=1, device_id={"query": lax.rem(q + k, nq)}, device_id_type=pl.DeviceIdType.MESH
        )
    for k in range(1, ni):
        pl.semaphore_signal(
            barrier, inc=1, device_id={"item": lax.rem(i + k, ni)}, device_id_type=pl.DeviceIdType.MESH
        )
    pl.semaphore_wait(barrier, nq + ni - 2)

    q_pos = y * gz + z
    query_copies = []
    for k in range(1, nq):
        there = lax.rem(q + k, nq)
        query_copies.append(send(query_ref, q_all.at[rows(q_pos * q_rows, q_rows)], {"query": there}))
    raw_copies = [send(raw_ref, raw_in.at[i], {"item": lax.rem(i + k, ni)}) for k in range(1, ni)]
    q_all[rows(q_pos * q_rows, q_rows), :] = query_ref[...]
    raw_in[i] = raw_ref[...]
    tokens = tokens_ref[...]
    pre = dot(tokens, w1_ref[...], (1, 0))
    pre_act[...] = pre
    finish(raw_copies)
    meta_rows = raw_ref.shape[0]
    parts = [raw_in[t, pl.ds(i, 1), :] for t in range(ni)] + [raw_ref[ni : ni + 1, :]]
    if meta_rows > ni + 1:
        parts.append(jnp.zeros((meta_rows - ni - 1, 128), jnp.int32))
    meta_in[q_pos] = jnp.concatenate(parts, axis=0)
    for k in range(1, nq):
        query_copies.append(send(meta_in.at[q_pos], meta_in.at[q_pos], {"query": lax.rem(q + k, nq)}))
    hidden[...] = jax.nn.silu(pre).astype(BF16)
    i_pos = core * gx + x
    emb_all[rows(i_pos * block, block), :] = dot(hidden[...], w2_ref[...], (1, 0)).astype(BF16)

    finish(gather_start(emb_all, core * gx * block, block, "x"))
    finish(gather_start(emb_all, 0, gx * block, "core"))

    finish(query_copies)
    lane = lax.broadcasted_iota(jnp.int32, (meta_rows, 128), 1)
    per = 128 // q_rows
    want_tiles, flag_tiles = [], []
    for t in range(nq // per):
        want = jnp.zeros((1, 128), jnp.int32)
        flag = jnp.zeros((meta_rows, 128), F32)
        for h in range(per):
            sent = meta_in[t * per + h]
            want = want + sent[ni : ni + 1, :]
            column = jnp.sum(jnp.where(lane == q, sent, 0).astype(F32), axis=1, keepdims=True)
            inside = (lane >= h * q_rows) & (lane < (h + 1) * q_rows)
            flag = flag + jnp.where(inside, column, 0.0)
        want_tiles.append(want)
        flag_tiles.append(flag)
    wanted = jnp.concatenate(want_tiles, axis=1)
    flags_all[...] = jnp.concatenate(flag_tiles, axis=1)

    def located(p):
        item = lax.rem(p, gx) * 2 + lax.div(p, gx)
        first = (item * nq + q) * block
        ids = lax.broadcasted_iota(jnp.int32, (block, n_q), 0)
        hit = ids == (wanted - first)
        live = flags_all[pl.ds(item, 1), :] > 0.5
        return hit, live

    def score_block(p, carried):
        top, total, positive = carried
        hit, live = located(p)
        s = 0.25 * dot(emb_all[rows(p * block, block), :], q_all[...], (1, 1))
        scores[rows(p * block, block), :] = s
        here = jnp.max(s, axis=0, keepdims=True)
        added = jnp.sum(jnp.exp(s - here), axis=0, keepdims=True)
        positive = positive + jnp.sum(jnp.where(hit, s, 0.0), axis=0, keepdims=True)
        here = jnp.where(live, here, -1e30)
        new_top = jnp.maximum(top, here)
        total = total * jnp.exp(top - new_top) + jnp.where(live, added * jnp.exp(here - new_top), 0.0)
        return new_top, total, positive

    start = (jnp.full((1, n_q), -1e30, F32), jnp.zeros((1, n_q), F32), jnp.zeros((1, n_q), F32))
    top, total, positive = lax.fori_loop(0, ni, score_block, start)
    stats_all[0] = jnp.concatenate([top, total, positive, jnp.zeros((5, n_q), F32)], axis=0)
    finish([
        send(stats_all.at[0], stats_all.at[k], {"query": lax.rem(q + k, nq)}) for k in range(1, nq)
    ])
    top = stats_all[0, 0:1, :]
    for k in range(1, nq):
        top = jnp.maximum(top, stats_all[k, 0:1, :])
    total = jnp.zeros((1, n_q), F32)
    positive = jnp.zeros((1, n_q), F32)
    for k in range(nq):
        total = total + stats_all[k, 1:2, :] * jnp.exp(stats_all[k, 0:1, :] - top)
        positive = positive + stats_all[k, 2:3, :]
    log_norm = top + jnp.log(total)
    loss_ref[...] = log_norm - positive

    def grad_block(p, carried):
        hit, live = located(p)
        s = scores[rows(p * block, block), :]
        weights = jnp.where(live, jnp.exp(s - log_norm), 0.0)
        c = (weights - hit.astype(F32)).astype(BF16)
        coeffs[rows(p * block, block), :] = c
        e_acc[rows(p * block, block), :] = 0.25 * dot(c, q_all[...], (1, 0))
        return carried

    lax.fori_loop((1 - core) * gx, (2 - core) * gx, grad_block, 0)
    e_copies = reduce_start(e_acc, e_recv_c, 0, gx * block, "core")
    lax.fori_loop(core * gx, (core + 1) * gx, grad_block, 0)
    e_base = reduce_finish(e_copies, e_acc, e_recv_c, 0, gx * block, "core")
    e_copies = reduce_start(e_acc, e_recv_x, e_base, block, "x")
    q_acc[...] = 0.25 * dot(coeffs[...], emb_all[...], (0, 0))
    q_copies = reduce_start(q_acc, q_recv_y, 0, gz * q_rows, "y")
    e_base = reduce_finish(e_copies, e_acc, e_recv_x, e_base, block, "x")
    own_grad = e_acc[rows(e_base, block), :].astype(BF16)

    hid, din = w2_ref.shape[0], tokens.shape[1]
    part = b_acc.shape[0]
    chains = [
        {"acc": a_acc, "out": a_out, "first": 0, "order": ("core", "x", "y", "z")},
        {"acc": a_acc, "out": a_out, "first": part, "order": ("core", "y", "x", "z")},
        {"acc": b_acc, "out": b_out, "first": 0, "order": ("core", "z", "x", "y")},
    ]
    landing = {"core": core_recv, "x": x_recv, "y": y_recv, "z": z_recv}

    def descend(n):
        chain = chains[n]
        level = chain.setdefault("level", 0)
        if level == 0:
            chain["base"], chain["size"] = chain["first"], part
        else:
            chain["base"] = reduce_finish(
                chain["copies"], chain["acc"], landing[chain["order"][level - 1]].at[n],
                chain["base"], chain["size"], chain["order"][level - 1],
            )
        if level < 4:
            axis = chain["order"][level]
            chain["size"] = chain["size"] // axes[axis][0]
            chain["copies"] = reduce_start(
                chain["acc"], landing[axis].at[n], chain["base"], chain["size"], axis
            )
            chain["level"] = level + 1
        else:
            here = rows(chain["base"], chain["size"])
            chain["out"][here, :] = (chain["acc"][here, :] * grad_scale).astype(chain["out"].dtype)
            chain["copies"] = []

    def ascend(n):
        chain = chains[n]
        finish(chain["copies"])
        level = chain["level"] - 1
        chain["level"] = level
        if level < 0:
            return
        group, own, _ = axes[chain["order"][level]]
        chain["base"] = chain["base"] - own * chain["size"]
        chain["copies"] = gather_start(
            chain["out"], chain["base"], chain["size"], chain["order"][level]
        )
        chain["size"] = chain["size"] * group

    second = dot(hidden[...], own_grad, (0, 0))
    for j in range(width // 128):
        b_acc[j * hid : (j + 1) * hid, :] = second[:, j * 128 : (j + 1) * 128]
    descend(2)
    hid_grad = dot(own_grad, w2_ref[...], (1, 1))
    pre = pre_act[...]
    sig = jax.nn.sigmoid(pre)
    pre_grad = (hid_grad * sig * (1.0 + pre * (1.0 - sig))).astype(BF16)
    half = hid // 2
    for n in range(2):
        first = dot(tokens, pre_grad[:, n * half : (n + 1) * half], (0, 0))
        for j in range(half // 128):
            start_row = n * part + j * din
            a_acc[start_row : start_row + din, :] = first[:, j * 128 : (j + 1) * 128]
        descend(n)
        if n == 0:
            descend(2)
            q_base = reduce_finish(q_copies, q_acc, q_recv_y, 0, gz * q_rows, "y")
            q_copies = reduce_start(q_acc, q_recv_z, q_base, q_rows, "z")
    for n in (0, 1, 0, 1, 2):
        descend(n)
    q_base = reduce_finish(q_copies, q_acc, q_recv_z, q_base, q_rows, "z")
    qgrad_ref[...] = q_acc[rows(q_base, q_rows), :]
    for n in (0, 1, 2):
        descend(n)
    descend(2)
    ascend(2)
    for n in (0, 1):
        descend(n)
        ascend(n)
    for n in (2, 0, 1, 2, 0, 1, 0, 1, 2, 0, 1, 2):
        ascend(n)


def on_device(query_emb, targets, eligible_tiles, item_feats, w_first, w_second):
    q_rows, width = query_emb.shape
    ni, nq = lax.axis_size("item"), lax.axis_size("query")
    gx, gz = ni // 2, nq // 2
    i, q = lax.axis_index("item"), lax.axis_index("query")
    tokens = item_feats.reshape(item_feats.shape[1], item_feats.shape[2])
    block, din = tokens.shape
    hid = w_first.shape[1]
    n_q = nq * q_rows
    q_pos = (q % 2) * gz + q // 2
    meta_rows = -(-(ni + 1) // 8) * 8
    per = 128 // q_rows
    own = lax.dynamic_slice_in_dim(targets, i * q_rows, q_rows, 0)
    mine = jnp.arange(128, dtype=jnp.int32) // q_rows == q_pos % per
    flags = jnp.pad((eligible_tiles > 0).astype(jnp.int32), ((0, meta_rows - ni), (0, 128 - nq)))
    at_row = jnp.arange(meta_rows, dtype=jnp.int32)[:, None] == ni
    raw = jnp.where(at_row, jnp.where(mine, jnp.tile(own, per), 0)[None, :], flags)

    a_rows, b_rows = din * hid // 128, hid * width // 128
    part = b_rows
    out_dtype = BF16 if part // (nq * ni) % 16 == 0 else F32
    n_copies = 3 * (nq - 1) + (ni - 1) + 2 * gx + gx + gz + 3 * 2 * (2 + gx - 1 + gz - 1)
    vmem = pltpu.VMEM
    loss, query_grad, g1, g2 = pl.pallas_call(
        functools.partial(window_kernel, (nq, ni, 1.0 / math.sqrt(block * nq * ni))),
        out_shape=(
            jax.ShapeDtypeStruct((1, n_q), F32),
            jax.ShapeDtypeStruct((q_rows, width), F32),
            jax.ShapeDtypeStruct((a_rows, 128), out_dtype),
            jax.ShapeDtypeStruct((b_rows, 128), out_dtype),
        ),
        in_specs=[pl.BlockSpec(memory_space=vmem)] * 5,
        out_specs=(pl.BlockSpec(memory_space=vmem),) * 4,
        scratch_shapes=[
            vmem((n_q, width), BF16),
            vmem((ni, meta_rows, 128), jnp.int32),
            vmem((nq, meta_rows, 128), jnp.int32),
            vmem((ni * block, width), BF16),
            vmem((meta_rows, n_q), F32),
            vmem((ni * block, n_q), F32),
            vmem((ni * block, n_q), BF16),
            vmem((nq, 8, n_q), F32),
            vmem((ni * block, width), F32),
            vmem((gx * block, width), F32),
            vmem((max(gx - 1, 1) * block, width), F32),
            vmem((n_q, width), F32),
            vmem((gz * q_rows, width), F32),
            vmem((max(gz - 1, 1) * q_rows, width), F32),
            vmem((block, hid), F32),
            vmem((block, hid), BF16),
            vmem((a_rows, 128), F32),
            vmem((b_rows, 128), F32),
            vmem((3, part // 2, 128), F32),
            vmem((3, part // 2, 128), F32),
            vmem((3, part // 4, 128), F32),
            vmem((3, part // 2, 128), F32),
            pltpu.SemaphoreType.DMA((n_copies,)),
            pltpu.SemaphoreType.DMA((n_copies,)),
        ],
        compiler_params=pltpu.CompilerParams(
            collective_id=0, has_side_effects=True, vmem_limit_bytes=58 * 2**20
        ),
        name="loss_window",
    )(query_emb, raw, tokens, w_first, w_second)
    loss = lax.dynamic_slice_in_dim(loss.reshape(n_q), q_pos * q_rows, q_rows, 0)
    g1 = g1.reshape(hid // 128, din, 128).transpose(1, 0, 2).reshape(din, hid).astype(F32)
    g2 = g2.reshape(width // 128, hid, 128).transpose(1, 0, 2).reshape(hid, width).astype(F32)
    return (loss, query_grad, g1, g2)


def solution(mesh):
    return jax.shard_map(
        on_device,
        mesh=mesh,
        in_specs=(
            P(("query", "item"), None),
            P("query"),
            P("query", "item"),
            P("item", "query", None),
            P(),
            P(),
        ),
        out_specs=(P(("query", "item")), P(("query", "item"), None), P(), P()),
        check_vma=False,
    )
```

time: 101 us -> 87.2 us (0.86)
  Pallas kernels: 90.6 us -> 78.3 us
  local copies, waits for them, and re-layouts: 8.04 us -> 2.78 us
  other arithmetic: 1.43 us -> 5.25 us
    pallas_call x1, Pallas kernels: 90.6 us -> 78.3 us  [on_device(): pl.pallas_call(functools.partial(window_kernel, (nq, ni, 1.0 / math.sqrt(...]
    unnamed x5, local copies, waits for them, and re-layouts: 5.69 us -> 0.64 us
    convert_element_type x1 -> x2, other arithmetic: 0.01 us -> 3.88 us  [the longest x1 2.84 us: on_device(): g1.reshape(hid // 128, din, 128).transpose(1, 0, 2).reshape(din, hid)]
where the time goes in v3:
time: 87.2 us; the launch traced here: 87 us
  Pallas kernels  78.3 us (90%)
  other arithmetic  5.25 us (6%)
  local copies, waits for them, and re-layouts  2.78 us (3%)
    pallas_call x1, Pallas kernels, on_device(): pl.pallas_call(functools.partial(window_kernel, (nq, ni, 1.0 / math.sqrt(...  78.3 us
    convert_element_type x1, other arithmetic, on_device(): g1.reshape(hid // 128, din, 128).transpose(1, 0, 2).reshape(din, hid)  2.84 us

profile of v3, /device:TPU:0, one launch (start us, length us, event | category | flops | bytes accessed | tf_op | source)
XLA Modules:
  0.0 87.0 jit_solution(13223976512161636976)
XLA Ops:
  0.6 0.7 broadcast_compare_fusion
  1.3 0.8 dynamic_slice.8
  2.1 0.1 tile.10
  2.2 0.7 convert_select_fusion.raw_ref
  2.8 78.3 %loss_window.1 = (f32[1,512]{1,0:T(1,128)}, f32[64,256]{1,0:T(8,128)}, bf16[4096,128]{1,0:T(8,128)(2,1)}, bf16[2048,128]{1,0:T(8,128)(2,1)}) custom-call(bf16[64,256]{1,0:T(8,128)(2,1)} %query_ref.1, s32[8,128]{1,0:T(8,128)} %convert_select_fusion.raw_ref, bf16[256,512]{1,0:T(8,128)(2,1)} %bitcast.21, bf16[512,1024]{1,0:T(8,128)(2,1)} %w1_ref.1, ...), custom_call_target="tpu_custom_call" | custom-call | tf_op jit(solution)/shard_map/loss_window/pallas_call | solution.py:302
  81.2 0.0 copy-start
  81.2 1.3 %dynamic-slice_bitcast_fusion = f32[64]{0:T(128)} fusion(f32[1,512]{1,0:T(1,128)} %get-tuple-element.8, s32[]{:T(128)S(6)} %select_n.49), kind=kLoop, calls=%fused_computation.11 | loop fusion | bytes 516 | tf_op jit(solution)/shard_map/dynamic_slice | solution.py:343
  82.5 0.0 copy-start.1
  82.5 2.8 %copy_bitcast_fusion = f32[512,1024]{1,0:T(8,128)} fusion(bf16[8,512,128]{2,1,0:T(8,128)(2,1)} %bitcast.19), kind=kLoop, calls=%fused_computation | loop fusion | flops 524288 | bytes 3145728 | tf_op jit(solution)/shard_map/convert_element_type | solution.py:344
  85.3 0.0 copy-done
  85.3 1.0 %copy_bitcast_fusion.1 = f32[1024,256]{1,0:T(8,128)} fusion(bf16[2,1024,128]{2,1,0:T(8,128)(2,1)S(1)} %bitcast.20), kind=kLoop, calls=%fused_computation.2 | loop fusion | flops 262144 | bytes 1572864 | tf_op jit(solution)/shard_map/convert_element_type | solution.py:345
  86.4 0.0 copy-done.1
  86.4 0.6 copy.17
  (3 shorter events, 0.0 us)
Async XLA Ops:
  81.2 4.2 %copy-start = (bf16[2048,128]{1,0:T(8,128)(2,1)S(1)}, bf16[2048,128]{1,0:T(8,128)(2,1)}, u32[]{:S(2)}) copy-start(bf16[2048,128]{1,0:T(8,128)(2,1)} %get-tuple-element.11) | copy-start | bytes 1572868
  82.5 3.9 %copy-start.1 = (f32[64,256]{1,0:T(8,128)S(1)}, f32[64,256]{1,0:T(8,128)}, u32[]{:S(2)}) copy-start(f32[64,256]{1,0:T(8,128)} %get-tuple-element.17) | copy-start | bytes 196612

commit v4 on v3

--- a/solution.py
+++ b/solution.py
@@ -22,22 +22,30 @@
 
 def window_kernel(
     shape,
-    query_ref, raw_ref, tokens_ref, w1_ref, w2_ref,
+    query_ref, targets_ref, flags_ref, tokens_hbm, w1_hbm, w2_hbm,
     loss_ref, qgrad_ref, a_out, b_out,
-    q_all, raw_in, meta_in, emb_all, flags_all, scores, coeffs, stats_all,
-    e_acc, e_recv_c, e_recv_x, q_acc, q_recv_y, q_recv_z,
-    pre_act, hidden, a_acc, b_acc, core_recv, x_recv, y_recv, z_recv,
-    send_sems, recv_sems,
+    tokens_ref, w1_ref, w2_ref, q_all, raw_in, meta_in, emb_all, flags_all, scores, coeffs, stats_all,
+    e_acc, e_recv_c, e_recv_x, q_acc, q_recv_y, q_recv_l, q_recv_h,
+    pre_act, hidden, a_acc, b_acc, core_recv, x_recv, y_recv, l_recv, h_recv,
+    send_sems, recv_sems, load_sems,
 ):
     nq, ni, grad_scale = shape
     gx, gz = ni // 2, nq // 2
     q, i = lax.axis_index("query"), lax.axis_index("item")
     core, x = lax.rem(i, 2), lax.div(i, 2)
     y, z = lax.rem(q, 2), lax.div(q, 2)
+    zl, zh = lax.rem(z, 2), lax.div(z, 2)
+    gh = gz // 2
     q_rows, width = query_ref.shape
     n_q = nq * q_rows
     block = tokens_ref.shape[0]
     used = [0]
+    loads = [
+        pltpu.make_async_copy(src, dst, load_sems.at[n])
+        for n, (src, dst) in enumerate(((tokens_hbm, tokens_ref), (w1_hbm, w1_ref), (w2_hbm, w2_ref)))
+    ]
+    for load in loads:
+        load.start()
 
     def send(src, dst, peer):
         slot = used[0]
@@ -57,7 +65,8 @@
         "core": (2, core, lambda t: {"item": x * 2 + t}),
         "x": (gx, x, lambda t: {"item": t * 2 + core}),
         "y": (2, y, lambda t: {"query": z * 2 + t}),
-        "z": (gz, z, lambda t: {"query": t * 2 + y}),
+        "zl": (2, zl, lambda t: {"query": (zh * 2 + t) * 2 + y}),
+        "zh": (gh, zh, lambda t: {"query": (t * 2 + zl) * 2 + y}),
     }
 
     def reduce_start(acc, recv, base, size, axis):
@@ -96,25 +105,39 @@
         )
     pl.semaphore_wait(barrier, nq + ni - 2)
 
-    q_pos = y * gz + z
+    q_pos = (y * 2 + zl) * gh + zh
     query_copies = []
     for k in range(1, nq):
         there = lax.rem(q + k, nq)
         query_copies.append(send(query_ref, q_all.at[rows(q_pos * q_rows, q_rows)], {"query": there}))
-    raw_copies = [send(raw_ref, raw_in.at[i], {"item": lax.rem(i + k, ni)}) for k in range(1, ni)]
+    per = 128 // q_rows
+    meta_rows = raw_in.shape[1]
+    raw_in[i] = jnp.zeros((meta_rows, 128), jnp.int32)
+    raw_in[i, 0:ni, 0:nq] = (flags_ref[...] > 0).astype(jnp.int32)
+    raw_copies = [send(raw_in.at[i], raw_in.at[i], {"item": lax.rem(i + k, ni)}) for k in range(1, ni)]
     q_all[rows(q_pos * q_rows, q_rows), :] = query_ref[...]
-    raw_in[i] = raw_ref[...]
+    lane_row = lax.broadcasted_iota(jnp.int32, (1, 128), 1)
+    first_lane = pl.multiple_of(lax.div(i, per) * 128, 128)
+    found = targets_ref[:, pl.ds(first_lane, 128)]
+    shift = lax.rem(q_pos - i + per * nq * ni, per)
+    moved = found
+    for h in range(1, per):
+        moved = jnp.where(shift == h, pltpu.roll(found, h * q_rows, 1), moved)
+    inside = lax.div(lane_row, q_rows) == lax.rem(q_pos, per)
+    own_targets = jnp.where(inside, moved, 0)
+    loads[0].wait()
+    loads[1].wait()
     tokens = tokens_ref[...]
     pre = dot(tokens, w1_ref[...], (1, 0))
     pre_act[...] = pre
     finish(raw_copies)
-    meta_rows = raw_ref.shape[0]
-    parts = [raw_in[t, pl.ds(i, 1), :] for t in range(ni)] + [raw_ref[ni : ni + 1, :]]
+    parts = [raw_in[t, pl.ds(i, 1), :] for t in range(ni)] + [own_targets]
     if meta_rows > ni + 1:
         parts.append(jnp.zeros((meta_rows - ni - 1, 128), jnp.int32))
     meta_in[q_pos] = jnp.concatenate(parts, axis=0)
     for k in range(1, nq):
         query_copies.append(send(meta_in.at[q_pos], meta_in.at[q_pos], {"query": lax.rem(q + k, nq)}))
+    loads[2].wait()
     hidden[...] = jax.nn.silu(pre).astype(BF16)
     i_pos = core * gx + x
     emb_all[rows(i_pos * block, block), :] = dot(hidden[...], w2_ref[...], (1, 0)).astype(BF16)
@@ -124,7 +147,6 @@
 
     finish(query_copies)
     lane = lax.broadcasted_iota(jnp.int32, (meta_rows, 128), 1)
-    per = 128 // q_rows
     want_tiles, flag_tiles = [], []
     for t in range(nq // per):
         want = jnp.zeros((1, 128), jnp.int32)
@@ -176,7 +198,12 @@
         total = total + stats_all[k, 1:2, :] * jnp.exp(stats_all[k, 0:1, :] - top)
         positive = positive + stats_all[k, 2:3, :]
     log_norm = top + jnp.log(total)
-    loss_ref[...] = log_norm - positive
+    stats_all[0, 0:1, :] = log_norm - positive
+    found = stats_all[0, 0:1, pl.ds(pl.multiple_of(lax.div(q_pos, per) * 128, 128), 128)]
+    moved = found
+    for h in range(1, per):
+        moved = jnp.where(lax.rem(q_pos, per) == h, pltpu.roll(found, (per - h) * q_rows, 1), moved)
+    loss_ref[...] = moved[:, :q_rows]
 
     def grad_block(p, carried):
         hit, live = located(p)
@@ -187,24 +214,36 @@
         e_acc[rows(p * block, block), :] = 0.25 * dot(c, q_all[...], (1, 0))
         return carried
 
-    lax.fori_loop((1 - core) * gx, (2 - core) * gx, grad_block, 0)
-    e_copies = reduce_start(e_acc, e_recv_c, 0, gx * block, "core")
-    lax.fori_loop(core * gx, (core + 1) * gx, grad_block, 0)
-    e_base = reduce_finish(e_copies, e_acc, e_recv_c, 0, gx * block, "core")
-    e_copies = reduce_start(e_acc, e_recv_x, e_base, block, "x")
+    e_size = gx * block
+    pairs = []
+    for k in list(range(1, gx)) + [0]:
+        t = lax.rem(x + k, gx)
+        grad_block((1 - core) * gx + t, 0)
+        leaving = rows(((1 - core) * gx + t) * block, block)
+        landed = e_recv_c.at[rows(t * block, block)]
+        pairs.append(send(e_acc.at[leaving], landed, {"item": x * 2 + 1 - core}))
+        grad_block(core * gx + t, 0)
+        if k > 0:
+            here = rows((core * gx + t) * block, block)
+            pairs[-1].wait()
+            e_acc[here, :] = e_acc[here, :] + e_recv_c[rows(t * block, block), :]
+            pairs[-1] = send(e_acc.at[here], e_recv_x.at[rows((k - 1) * block, block)], {"item": t * 2 + core})
     q_acc[...] = 0.25 * dot(coeffs[...], emb_all[...], (0, 0))
     q_copies = reduce_start(q_acc, q_recv_y, 0, gz * q_rows, "y")
-    e_base = reduce_finish(e_copies, e_acc, e_recv_x, e_base, block, "x")
+    e_base = (core * gx + x) * block
+    pairs[-1].wait()
+    e_acc[rows(e_base, block), :] = e_acc[rows(e_base, block), :] + e_recv_c[rows(x * block, block), :]
+    e_base = reduce_finish(pairs[:-1], e_acc, e_recv_x, core * gx * block, block, "x")
     own_grad = e_acc[rows(e_base, block), :].astype(BF16)
 
     hid, din = w2_ref.shape[0], tokens.shape[1]
     part = b_acc.shape[0]
     chains = [
-        {"acc": a_acc, "out": a_out, "first": 0, "order": ("core", "x", "y", "z")},
-        {"acc": a_acc, "out": a_out, "first": part, "order": ("core", "y", "x", "z")},
-        {"acc": b_acc, "out": b_out, "first": 0, "order": ("core", "z", "x", "y")},
+        {"acc": a_acc, "out": a_out, "first": 0, "order": ("core", "x", "y", "zl", "zh")},
+        {"acc": a_acc, "out": a_out, "first": part, "order": ("core", "y", "x", "zl", "zh")},
+        {"acc": b_acc, "out": b_out, "first": 0, "order": ("core", "zl", "zh", "x", "y")},
     ]
-    landing = {"core": core_recv, "x": x_recv, "y": y_recv, "z": z_recv}
+    landing = {"core": core_recv, "x": x_recv, "y": y_recv, "zl": l_recv, "zh": h_recv}
 
     def descend(n):
         chain = chains[n]
@@ -216,7 +255,7 @@
                 chain["copies"], chain["acc"], landing[chain["order"][level - 1]].at[n],
                 chain["base"], chain["size"], chain["order"][level - 1],
             )
-        if level < 4:
+        if level < 5:
             axis = chain["order"][level]
             chain["size"] = chain["size"] // axes[axis][0]
             chain["copies"] = reduce_start(
@@ -246,6 +285,8 @@
     for j in range(width // 128):
         b_acc[j * hid : (j + 1) * hid, :] = second[:, j * 128 : (j + 1) * 128]
     descend(2)
+    q_base = reduce_finish(q_copies, q_acc, q_recv_y, 0, gz * q_rows, "y")
+    q_copies = reduce_start(q_acc, q_recv_l, q_base, gh * q_rows, "zl")
     hid_grad = dot(own_grad, w2_ref[...], (1, 1))
     pre = pre_act[...]
     sig = jax.nn.sigmoid(pre)
@@ -259,20 +300,19 @@
         descend(n)
         if n == 0:
             descend(2)
-            q_base = reduce_finish(q_copies, q_acc, q_recv_y, 0, gz * q_rows, "y")
-            q_copies = reduce_start(q_acc, q_recv_z, q_base, q_rows, "z")
-    for n in (0, 1, 0, 1, 2):
+            q_base = reduce_finish(q_copies, q_acc, q_recv_l, q_base, gh * q_rows, "zl")
+            q_copies = reduce_start(q_acc, q_recv_h, q_base, q_rows, "zh")
+    for n in (0, 1, 2, 0, 1):
         descend(n)
-    q_base = reduce_finish(q_copies, q_acc, q_recv_z, q_base, q_rows, "z")
+    q_base = reduce_finish(q_copies, q_acc, q_recv_h, q_base, q_rows, "zh")
     qgrad_ref[...] = q_acc[rows(q_base, q_rows), :]
-    for n in (0, 1, 2):
+    for n in (2, 0, 1, 2, 0, 1, 2):
         descend(n)
-    descend(2)
     ascend(2)
     for n in (0, 1):
         descend(n)
         ascend(n)
-    for n in (2, 0, 1, 2, 0, 1, 0, 1, 2, 0, 1, 2):
+    for n in (2, 0, 1, 2, 0, 1, 2, 0, 1, 2, 0, 1, 2, 0, 1):
         ascend(n)
 
 
@@ -280,36 +320,30 @@
     q_rows, width = query_emb.shape
     ni, nq = lax.axis_size("item"), lax.axis_size("query")
     gx, gz = ni // 2, nq // 2
-    i, q = lax.axis_index("item"), lax.axis_index("query")
     tokens = item_feats.reshape(item_feats.shape[1], item_feats.shape[2])
     block, din = tokens.shape
     hid = w_first.shape[1]
     n_q = nq * q_rows
-    q_pos = (q % 2) * gz + q // 2
     meta_rows = -(-(ni + 1) // 8) * 8
-    per = 128 // q_rows
-    own = lax.dynamic_slice_in_dim(targets, i * q_rows, q_rows, 0)
-    mine = jnp.arange(128, dtype=jnp.int32) // q_rows == q_pos % per
-    flags = jnp.pad((eligible_tiles > 0).astype(jnp.int32), ((0, meta_rows - ni), (0, 128 - nq)))
-    at_row = jnp.arange(meta_rows, dtype=jnp.int32)[:, None] == ni
-    raw = jnp.where(at_row, jnp.where(mine, jnp.tile(own, per), 0)[None, :], flags)
-
     a_rows, b_rows = din * hid // 128, hid * width // 128
     part = b_rows
     out_dtype = BF16 if part // (nq * ni) % 16 == 0 else F32
-    n_copies = 3 * (nq - 1) + (ni - 1) + 2 * gx + gx + gz + 3 * 2 * (2 + gx - 1 + gz - 1)
+    n_copies = 3 * (nq - 1) + (ni - 1) + 2 * gx + gx + gz + 3 * 2 * (3 + gx - 1 + gz // 2 - 1)
     vmem = pltpu.VMEM
     loss, query_grad, g1, g2 = pl.pallas_call(
         functools.partial(window_kernel, (nq, ni, 1.0 / math.sqrt(block * nq * ni))),
         out_shape=(
-            jax.ShapeDtypeStruct((1, n_q), F32),
+            jax.ShapeDtypeStruct((1, q_rows), F32),
             jax.ShapeDtypeStruct((q_rows, width), F32),
             jax.ShapeDtypeStruct((a_rows, 128), out_dtype),
             jax.ShapeDtypeStruct((b_rows, 128), out_dtype),
         ),
-        in_specs=[pl.BlockSpec(memory_space=vmem)] * 5,
+        in_specs=[pl.BlockSpec(memory_space=vmem)] * 3 + [pl.BlockSpec(memory_space=pl.ANY)] * 3,
         out_specs=(pl.BlockSpec(memory_space=vmem),) * 4,
         scratch_shapes=[
+            vmem((block, din), BF16),
+            vmem((din, hid), BF16),
+            vmem((hid, width), BF16),
             vmem((n_q, width), BF16),
             vmem((ni, meta_rows, 128), jnp.int32),
             vmem((nq, meta_rows, 128), jnp.int32),
@@ -323,7 +357,8 @@
             vmem((max(gx - 1, 1) * block, width), F32),
             vmem((n_q, width), F32),
             vmem((gz * q_rows, width), F32),
-            vmem((max(gz - 1, 1) * q_rows, width), F32),
+            vmem((gz // 2 * q_rows, width), F32),
+            vmem((max(gz // 2 - 1, 1) * q_rows, width), F32),
             vmem((block, hid), F32),
             vmem((block, hid), BF16),
             vmem((a_rows, 128), F32),
@@ -331,16 +366,18 @@
             vmem((3, part // 2, 128), F32),
             vmem((3, part // 2, 128), F32),
             vmem((3, part // 4, 128), F32),
-            vmem((3, part // 2, 128), F32),
+            vmem((3, part // 4, 128), F32),
+            vmem((3, part // 4, 128), F32),
             pltpu.SemaphoreType.DMA((n_copies,)),
             pltpu.SemaphoreType.DMA((n_copies,)),
+            pltpu.SemaphoreType.DMA((3,)),
         ],
         compiler_params=pltpu.CompilerParams(
             collective_id=0, has_side_effects=True, vmem_limit_bytes=58 * 2**20
         ),
         name="loss_window",
-    )(query_emb, raw, tokens, w_first, w_second)
-    loss = lax.dynamic_slice_in_dim(loss.reshape(n_q), q_pos * q_rows, q_rows, 0)
+    )(query_emb, targets.reshape(1, -1), eligible_tiles, tokens, w_first, w_second)
+    loss = loss.reshape(q_rows)
     g1 = g1.reshape(hid // 128, din, 128).transpose(1, 0, 2).reshape(din, hid).astype(F32)
     g2 = g2.reshape(width // 128, hid, 128).transpose(1, 0, 2).reshape(hid, width).astype(F32)
     return (loss, query_grad, g1, g2)

time: 87.2 us -> 83.7 us (0.960)
  local copies, waits for them, and re-layouts: 2.78 us -> 1.15 us
  other arithmetic: 5.25 us -> 3.91 us
    dynamic_slice x2 -> x0, local copies, waits for them, and re-layouts: 2.06 us -> none  [the longest x1 1.31 us: on_device(): lax.dynamic_slice_in_dim(loss.reshape(n_q), q_pos * q_rows, q_rows, 0)]
where the time goes in v4:
time: 83.7 us; the launch traced here: 83.5 us
  Pallas kernels  77.8 us (93%)
  other arithmetic  3.91 us (5%)
  local copies, waits for them, and re-layouts  1.15 us (1%)
    pallas_call x1, Pallas kernels, on_device(): pl.pallas_call(functools.partial(window_kernel, (nq, ni, 1.0 / math.sqrt(...  77.8 us
    convert_element_type x1, other arithmetic, on_device(): g1.reshape(hid // 128, din, 128).transpose(1, 0, 2).reshape(din, hid)  2.87 us

profile of v4, /device:TPU:0, one launch (start us, length us, event | category | flops | bytes accessed | tf_op | source)
XLA Modules:
  0.0 83.5 jit_solution(3156335602083892730)
XLA Ops:
  0.6 77.8 %loss_window.1 = (f32[1,64]{1,0:T(1,128)}, f32[64,256]{1,0:T(8,128)}, bf16[4096,128]{1,0:T(8,128)(2,1)}, bf16[2048,128]{1,0:T(8,128)(2,1)}) custom-call(bf16[64,256]{1,0:T(8,128)(2,1)} %query_ref.1, s32[1,256]{1,0:T(1,128)} %bitcast.22, s32[4,8]{1,0:T(4,128)} %flags_ref.1, bf16[256,512]{1,0:T(8,128)(2,1)} %bitcast.21, bf16[512,1024]{1,0:T(8,128)(2,1)} %w1_hbm.1, ...), custom_call_target="tpu_custom_call" | custom-call | tf_op jit(solution)/shard_map/loss_window/pallas_call | solution.py:333
  78.4 0.0 copy-start
  78.4 0.0 copy-start.2
  78.4 0.0 copy-start.1
  78.5 2.9 %copy_bitcast_fusion = f32[512,1024]{1,0:T(8,128)} fusion(bf16[8,512,128]{2,1,0:T(8,128)(2,1)} %bitcast.19), kind=kLoop, calls=%fused_computation | loop fusion | flops 524288 | bytes 3145728 | tf_op jit(solution)/shard_map/convert_element_type | solution.py:381
  81.3 0.0 copy-done
  81.3 1.0 %copy_bitcast_fusion.1 = f32[1024,256]{1,0:T(8,128)} fusion(bf16[2,1024,128]{2,1,0:T(8,128)(2,1)S(1)} %bitcast.20), kind=kLoop, calls=%fused_computation.2 | loop fusion | flops 262144 | bytes 1572864 | tf_op jit(solution)/shard_map/convert_element_type | solution.py:382
  82.4 0.0 copy-done.2
  82.4 0.5 copy.18
  82.9 0.0 copy-done.1
  82.9 0.6 copy.19
Async XLA Ops:
  78.4 2.9 %copy-start = (bf16[2048,128]{1,0:T(8,128)(2,1)S(1)}, bf16[2048,128]{1,0:T(8,128)(2,1)}, u32[]{:S(2)}) copy-start(bf16[2048,128]{1,0:T(8,128)(2,1)} %get-tuple-element.11) | copy-start | bytes 1572868
  78.4 3.9 %copy-start.2 = (f32[1,64]{1,0:T(1,128)S(1)}, f32[1,64]{1,0:T(1,128)}, u32[]{:S(2)}) copy-start(f32[1,64]{1,0:T(1,128)} %get-tuple-element.8) | copy-start | bytes 772
  78.4 4.4 %copy-start.1 = (f32[64,256]{1,0:T(8,128)S(1)}, f32[64,256]{1,0:T(8,128)}, u32[]{:S(2)}) copy-start(f32[64,256]{1,0:T(8,128)} %get-tuple-element.17) | copy-start | bytes 196612

commit v5 on v4

--- a/solution.py
+++ b/solution.py
@@ -65,6 +65,7 @@
         "core": (2, core, lambda t: {"item": x * 2 + t}),
         "x": (gx, x, lambda t: {"item": t * 2 + core}),
         "y": (2, y, lambda t: {"query": z * 2 + t}),
+        "z": (gz, z, lambda t: {"query": t * 2 + y}),
         "zl": (2, zl, lambda t: {"query": (zh * 2 + t) * 2 + y}),
         "zh": (gh, zh, lambda t: {"query": (t * 2 + zl) * 2 + y}),
     }
@@ -239,11 +240,11 @@
     hid, din = w2_ref.shape[0], tokens.shape[1]
     part = b_acc.shape[0]
     chains = [
-        {"acc": a_acc, "out": a_out, "first": 0, "order": ("core", "x", "y", "zl", "zh")},
-        {"acc": a_acc, "out": a_out, "first": part, "order": ("core", "y", "x", "zl", "zh")},
+        {"acc": a_acc, "out": a_out, "first": 0, "order": ("core", "x", "y", "z")},
+        {"acc": a_acc, "out": a_out, "first": part, "order": ("core", "y", "x", "z")},
         {"acc": b_acc, "out": b_out, "first": 0, "order": ("core", "zl", "zh", "x", "y")},
     ]
-    landing = {"core": core_recv, "x": x_recv, "y": y_recv, "zl": l_recv, "zh": h_recv}
+    landing = {"core": core_recv, "x": x_recv, "y": y_recv, "zl": l_recv, "zh": h_recv, "z": h_recv}
 
     def descend(n):
         chain = chains[n]
@@ -255,7 +256,7 @@
                 chain["copies"], chain["acc"], landing[chain["order"][level - 1]].at[n],
                 chain["base"], chain["size"], chain["order"][level - 1],
             )
-        if level < 5:
+        if level < len(chain["order"]):
             axis = chain["order"][level]
             chain["size"] = chain["size"] // axes[axis][0]
             chain["copies"] = reduce_start(
@@ -306,13 +307,13 @@
         descend(n)
     q_base = reduce_finish(q_copies, q_acc, q_recv_h, q_base, q_rows, "zh")
     qgrad_ref[...] = q_acc[rows(q_base, q_rows), :]
-    for n in (2, 0, 1, 2, 0, 1, 2):
+    for n in (0, 1, 2, 2, 2):
         descend(n)
     ascend(2)
     for n in (0, 1):
         descend(n)
         ascend(n)
-    for n in (2, 0, 1, 2, 0, 1, 2, 0, 1, 2, 0, 1, 2, 0, 1):
+    for n in (2, 0, 1, 2, 0, 1, 2, 0, 1, 2, 0, 1, 2):
         ascend(n)
 
 
@@ -328,7 +329,7 @@
     a_rows, b_rows = din * hid // 128, hid * width // 128
     part = b_rows
     out_dtype = BF16 if part // (nq * ni) % 16 == 0 else F32
-    n_copies = 3 * (nq - 1) + (ni - 1) + 2 * gx + gx + gz + 3 * 2 * (3 + gx - 1 + gz // 2 - 1)
+    n_copies = 3 * (nq - 1) + (ni - 1) + 2 * gx + gx + gz + 3 * 2 * (3 + gx - 1 + gz - 1)
     vmem = pltpu.VMEM
     loss, query_grad, g1, g2 = pl.pallas_call(
         functools.partial(window_kernel, (nq, ni, 1.0 / math.sqrt(block * nq * ni))),

time: 83.7 us -> 82 us (0.980)
  Pallas kernels: 77.8 us -> 76 us
    pallas_call x1, Pallas kernels: 77.8 us -> 76 us  [on_device(): pl.pallas_call(functools.partial(window_kernel, (nq, ni, 1.0 / math.sqrt(...]
where the time goes in v5:
time: 82 us; the launch traced here: 81.8 us
  Pallas kernels  76 us (93%)
  other arithmetic  3.91 us (5%)
  local copies, waits for them, and re-layouts  1.15 us (1%)
    pallas_call x1, Pallas kernels, on_device(): pl.pallas_call(functools.partial(window_kernel, (nq, ni, 1.0 / math.sqrt(...  76 us
    convert_element_type x1, other arithmetic, on_device(): g1.reshape(hid // 128, din, 128).transpose(1, 0, 2).reshape(din, hid)  2.87 us

profile of v5, /device:TPU:0, one launch (start us, length us, event | category | flops | bytes accessed | tf_op | source)
XLA Modules:
  0.0 81.8 jit_solution(4185553744196672556)
XLA Ops:
  0.6 76.0 %loss_window.1 = (f32[1,64]{1,0:T(1,128)}, f32[64,256]{1,0:T(8,128)}, bf16[4096,128]{1,0:T(8,128)(2,1)}, bf16[2048,128]{1,0:T(8,128)(2,1)}) custom-call(bf16[64,256]{1,0:T(8,128)(2,1)} %query_ref.1, s32[1,256]{1,0:T(1,128)} %bitcast.22, s32[4,8]{1,0:T(4,128)} %flags_ref.1, bf16[256,512]{1,0:T(8,128)(2,1)} %bitcast.21, bf16[512,1024]{1,0:T(8,128)(2,1)} %w1_hbm.1, ...), custom_call_target="tpu_custom_call" | custom-call | tf_op jit(solution)/shard_map/loss_window/pallas_call | solution.py:334
  76.7 0.0 copy-start
  76.7 0.0 copy-start.2
  76.7 0.0 copy-start.1
  76.7 2.9 %copy_bitcast_fusion = f32[512,1024]{1,0:T(8,128)} fusion(bf16[8,512,128]{2,1,0:T(8,128)(2,1)} %bitcast.19), kind=kLoop, calls=%fused_computation | loop fusion | flops 524288 | bytes 3145728 | tf_op jit(solution)/shard_map/convert_element_type | solution.py:382
  79.6 0.0 copy-done
  79.6 1.0 %copy_bitcast_fusion.1 = f32[1024,256]{1,0:T(8,128)} fusion(bf16[2,1024,128]{2,1,0:T(8,128)(2,1)S(1)} %bitcast.20), kind=kLoop, calls=%fused_computation.2 | loop fusion | flops 262144 | bytes 1572864 | tf_op jit(solution)/shard_map/convert_element_type | solution.py:383
  80.6 0.0 copy-done.2
  80.6 0.5 copy.18
  81.1 0.0 copy-done.1
  81.1 0.6 copy.19
Async XLA Ops:
  76.7 2.9 %copy-start = (bf16[2048,128]{1,0:T(8,128)(2,1)S(1)}, bf16[2048,128]{1,0:T(8,128)(2,1)}, u32[]{:S(2)}) copy-start(bf16[2048,128]{1,0:T(8,128)(2,1)} %get-tuple-element.11) | copy-start | bytes 1572868
  76.7 3.9 %copy-start.2 = (f32[1,64]{1,0:T(1,128)S(1)}, f32[1,64]{1,0:T(1,128)}, u32[]{:S(2)}) copy-start(f32[1,64]{1,0:T(1,128)} %get-tuple-element.8) | copy-start | bytes 772
  76.7 4.4 %copy-start.1 = (f32[64,256]{1,0:T(8,128)S(1)}, f32[64,256]{1,0:T(8,128)}, u32[]{:S(2)}) copy-start(f32[64,256]{1,0:T(8,128)} %get-tuple-element.17) | copy-start | bytes 196612
